TPU v7x, 32 devices: a whole 2x2x4 slice. The times are simulated.
32 devices in a mesh: dp: 16 (over z, x, core), head: 2 (over y).
Axes of the slice: x: 2, y: 2, z: 4, core: 2. Of those that a mesh axis runs over, the one named last changes fastest.
Arguments:
- hidden_in: bfloat16 [8192, 768], P('dp'), may hold values from -6 to 6
- lengths: int32 [16], P('dp'), may hold values from 256 to 512
- cotangent: bfloat16 [8192, 768], P('dp'), may hold values from -6 to 6
- w_query: bfloat16 [768, 768], P(None, 'head'), may hold values from -0.21875 to 0.21875
- b_query: bfloat16 [768], P('head'), may hold values from -2 to 2
- w_key: bfloat16 [768, 768], P(None, 'head'), may hold values from -0.21875 to 0.21875
- b_key: bfloat16 [768], P('head'), may hold values from -2 to 2
- w_value: bfloat16 [768, 768], P(None, 'head'), may hold values from -0.21875 to 0.21875
- b_value: bfloat16 [768], P('head'), may hold values from -2 to 2
- w_out: bfloat16 [768, 768], P('head'), may hold values from -2.5 to 2.5
- b_out: bfloat16 [768], replicated, may hold values from -2 to 2
- ln1_gain: bfloat16 [768], replicated, may hold values from 0.5 to 1.5
- ln1_bias: bfloat16 [768], replicated, may hold values from -2 to 2
- w_in: bfloat16 [768, 3072], P(None, 'head'), may hold values from -0.21875 to 0.21875
- b_in: bfloat16 [3072], P('head'), may hold values from -2 to 2
- w_down: bfloat16 [3072, 768], P('head'), may hold values from -0.109375 to 0.109375
- b_down: bfloat16 [768], replicated, may hold values from -2 to 2
- ln2_gain: bfloat16 [768], replicated, may hold values from 0.5 to 1.5
- ln2_bias: bfloat16 [768], replicated, may hold values from -2 to 2
- rel_table: bfloat16 [512, 768], replicated, may hold values from -6 to 6
Outputs:
- output: bfloat16 [8192, 768], P('dp')
- grad_input: bfloat16 [8192, 768], P('dp')
- grad_w_query: float32 [768, 768], P('dp', 'head')
- grad_b_query: float32 [768], P('head')
- grad_w_key: float32 [768, 768], P('dp', 'head')
- grad_b_key: float32 [768], P('head')
- grad_w_value: float32 [768, 768], P('dp', 'head')
- grad_b_value: float32 [768], P('head')
- grad_w_out: float32 [768, 768], P('head', 'dp')
- grad_b_out: float32 [768], replicated
- grad_ln1_gain: float32 [768], replicated
- grad_ln1_bias: float32 [768], replicated
- grad_w_in: float32 [768, 3072], P('dp', 'head')
- grad_b_in: float32 [3072], P('head')
- grad_w_down: float32 [3072, 768], P('head', 'dp')
- grad_b_down: float32 [768], replicated
- grad_ln2_gain: float32 [768], replicated
- grad_ln2_bias: float32 [768], replicated
- grad_rel_table: float32 [512, 768], replicated
Inputs may be any that keep to these rules, and one draw needn't show every extreme that they name: The first lengths tokens of a row are real, the rest is padding.
All inputs are finite; a program needn't handle non-finite values.
Results may differ from a plain program's by a relative error of at most 0.024.
Values sent between devices are 32-bit elements; how exact they have to be, the bound alone decides.
No kernel may reach another device: no remote copies, remote signals or barrier semaphores. Data moves between devices by JAX's collectives and lax.ppermute only.
A program may use at most 192 MiB of HBM per device.

v0:
```python
import functools
import itertools
import math

import jax
import jax.numpy as jnp
import numpy as np
from jax import lax
from jax.experimental import pallas as pl
from jax.experimental.pallas import tpu as pltpu
from jax.sharding import PartitionSpec as P

HEAD_DIM = 64
SPAN = 256
MAXPOS = 512
EPSILON = 1e-07
MASKED = -1000000000.0
LANES = 128
STREAMS = 2
CONTEXTS = 1
TAIL = "YLKGDIR(VQ)RDVXISQJiQqP(VH)dP(vU)"
REL_PIECES = 1
HEAD_PIECES = 1
QUARTERS = 4
COLUMNS = 384
BACK_FLOPS = 64 << 30
STEP_FLOPS = 1024
GRAD_FLOPS = 1024
VMEM_LIMIT = 8 * 1024 * 1024

BF16 = jnp.bfloat16
F32 = jnp.float32


def bucket_of(offsets, bucket_span, max_distance):
    middle = bucket_span // 2
    direction = np.sign(offsets)
    absolute = np.where((offsets < middle) & (offsets > -middle), middle - 1, np.abs(offsets))
    log_part = (
        np.ceil(np.log(absolute / middle) / np.log((max_distance - 1) / middle) * (middle - 1))
        + middle
    )
    bucket = np.where(absolute <= middle, offsets, log_part * direction).astype(np.int64)
    return np.clip(bucket + bucket_span, 0, 2 * bucket_span - 1).astype(np.int32)


def distance_buckets(seq_len):
    offsets = np.maximum(seq_len - 1 - np.arange(2 * seq_len), 1 - seq_len)
    return bucket_of(offsets, SPAN, MAXPOS)


def dot_nn(a, b):
    return lax.dot_general(a, b, (((1,), (0,)), ((), ())), preferred_element_type=F32)


def dot_nt(a, b):
    return lax.dot_general(a, b, (((1,), (1,)), ((), ())), preferred_element_type=F32)


def dot_tn(a, b):
    return lax.dot_general(a, b, (((0,), (0,)), ((), ())), preferred_element_type=F32)


def resume(work, results):
    try:
        yield work.send(results)
    except StopIteration:
        return


class Line:
    def __init__(self):
        self.last = ()

    def call(
        self, kernel, name, outs, operands, aliases=None, scalars=0, scratch=(), flops=1024,
        space=pltpu.VMEM, direct=(),
    ):
        in_specs = [pl.BlockSpec(memory_space=pltpu.SMEM)] * scalars
        in_specs += [pl.BlockSpec(memory_space=space)] * (len(operands) - scalars)
        in_specs += [pl.BlockSpec(memory_space=pl.ANY)] * len(self.last)
        count, skipped = len(operands), len(self.last)

        def body(*refs):
            kernel(*refs[:count], *refs[count + skipped :])

        results = pl.pallas_call(
            body,
            in_specs=in_specs,
            out_specs=[
                pl.BlockSpec() if at in direct else pl.BlockSpec(memory_space=pltpu.VMEM)
                for at in range(len(outs))
            ],
            out_shape=outs,
            scratch_shapes=list(scratch),
            input_output_aliases=aliases or {},
            compiler_params=pltpu.CompilerParams(vmem_limit_bytes=VMEM_LIMIT),
            cost_estimate=pl.CostEstimate(flops=flops, bytes_accessed=1024, transcendentals=0),
            name=name,
        )(*operands, *self.last)
        self.last = (min(results, key=lambda result: result.size * result.dtype.itemsize),)
        return results


    def group(self, works):
        calls = [next(work) for work in works]
        ins = [len(call[3]) for call in calls]
        sizes = [len(call[2]) for call in calls]

        def kernel(*refs):
            in_refs, out_refs = refs[: sum(ins)], refs[sum(ins) :]
            for call, count, size in zip(calls, ins, sizes, strict=True):
                call[0](*in_refs[:count], *out_refs[:size])
                in_refs, out_refs = in_refs[count:], out_refs[size:]

        outs, operands, direct = [], [], []
        for _, _, call_outs, call_operands, call_direct in calls:
            direct += [len(outs) + at for at in call_direct]
            outs += call_outs
            operands += call_operands
        name = "__".join(call[1] for call in calls)
        results = self.call(kernel, name, outs, operands, direct=direct, flops=STEP_FLOPS)
        for work, size in zip(works, sizes, strict=True):
            part, results = results[:size], results[size:]
            for _ in itertools.islice(resume(work, part), 1):
                raise ValueError("second call")


def sds(shape, dtype):
    return jax.ShapeDtypeStruct(shape, dtype)


def onehot_of(bucket_ref, span):
    buckets = bucket_ref[...]
    hot = buckets == lax.broadcasted_iota(jnp.int32, (span, buckets.shape[1]), 0)
    return jnp.where(hot, 1.0, 0.0).astype(BF16)


def project_kernel(
    bucket_hbm, hidden_hbm, wq_hbm, bq_hbm, wk_hbm, bk_hbm, wv_hbm, bv_hbm, table_hbm, wout_hbm,
    q_ref, k_ref, v_ref, eq_ref, ek_ref, mine_ref,
    bucket_ref, hidden_ref, weight_ref, bq_ref, bk_ref, bv_ref, table_ref, quarter_ref, sems,
):
    rows = quarter_ref.shape[0]
    first = pl.multiple_of(lax.rem(lax.axis_index("dp"), QUARTERS) * rows, rows)
    cols = q_ref.shape[1]
    weights = [weight_ref.at[:, at * cols : (at + 1) * cols] for at in range(3)]
    sources = (
        wout_hbm.at[pl.ds(first, rows)], hidden_hbm, wq_hbm, wk_hbm, wv_hbm, bq_hbm, bk_hbm, bv_hbm,
        table_hbm, bucket_hbm,
    )
    targets = (
        quarter_ref, hidden_ref, *weights, bq_ref, bk_ref, bv_ref, table_ref, bucket_ref,
    )
    copies = [
        pltpu.make_async_copy(source, target, sems.at[at])
        for at, (source, target) in enumerate(zip(sources, targets, strict=True))
    ]
    for copy in copies:
        copy.start()
    copies[0].wait()
    mine_ref[...] = quarter_ref[...].astype(F32)
    for copy in copies[1:8]:
        copy.wait()
    bias = jnp.concatenate([ref[...].astype(F32)[None, :] for ref in (bq_ref, bk_ref, bv_ref)], axis=1)
    rows = (dot_nn(hidden_ref[...], weight_ref[...]) + bias).astype(BF16)
    for at, ref in enumerate((q_ref, k_ref, v_ref)):
        ref[...] = rows[:, at * cols : (at + 1) * cols]
    for copy in copies[8:]:
        copy.wait()
    table = table_ref[...]
    onehot = onehot_of(bucket_ref, table.shape[0])
    both = (dot_nn(table, weight_ref[:, : 2 * cols]) + bias[:, : 2 * cols]).astype(BF16)
    spread_out = dot_tn(onehot, both).astype(BF16)
    eq_ref[...] = spread_out[:, :cols]
    ek_ref[...] = spread_out[:, cols:]


def project(line, buckets, hidden, wq, bq, wk, bk, wv, bv, table, wout):
    seq_len = hidden.shape[0]
    cols = wq.shape[1]
    rows = wout.shape[0] // QUARTERS
    outs = [sds((seq_len, cols), BF16)] * 3 + [sds((2 * seq_len, cols), BF16)] * 2
    outs += [sds((rows, wout.shape[1]), F32)]
    operands = (buckets, hidden, wq, bq, wk, bk, wv, bv, table, wout)
    shapes = [buckets, hidden, sds((wq.shape[0], 3 * cols), wq.dtype), bq, bk, bv, table]
    scratch = [pltpu.VMEM(array.shape, array.dtype) for array in shapes]
    scratch += [pltpu.VMEM((rows, wout.shape[1]), wout.dtype)]
    operands = [pltpu.with_memory_space_constraint(operand, pltpu.HBM) for operand in operands]
    scratch += [pltpu.SemaphoreType.DMA((len(operands),))]
    return line.call(
        project_kernel, "project", outs, operands, scratch=scratch, space=pltpu.HBM
    )


def assemble_kernel(own_ref, *refs):
    out_ref = refs[-1]
    side, me = lax.axis_index("head"), lax.rem(lax.axis_index("dp"), QUARTERS)
    out_ref[side] = own_ref[...]
    for origin, ref in enumerate(refs[:-1]):
        rows = ref.shape[0]
        first = pl.multiple_of((me ^ origin) * rows, rows)
        out_ref[1 - side, pl.ds(first, rows), :] = ref[...].astype(BF16)


def assemble(line, own, quarters):
    rows, width = own.shape
    out = sds((2, rows, width), BF16)
    (joined,) = line.call(assemble_kernel, "assemble", [out], (own, *quarters))
    return joined.reshape(2 * rows, width)


def half_masks():
    lane = lax.broadcasted_iota(jnp.int32, (1, LANES), 1)
    return [lane // HEAD_DIM == side for side in range(LANES // HEAD_DIM)]


def apart(masks, value):
    zero = jnp.zeros_like(value)
    return jnp.concatenate([jnp.where(mask, value, zero) for mask in masks], axis=0)


def join(masks, stacked):
    rows = stacked.shape[0] // 2
    return jnp.where(masks[0], stacked[:rows], stacked[rows:])


def skewed(stacked, shift):
    rows = stacked.shape[0] // 2
    parts = [
        pltpu.roll(part, shift, 1, stride=1, stride_axis=0)
        for part in (stacked[:rows], stacked[rows:])
    ]
    return jnp.concatenate(parts, axis=0)


def attend_kernel(at, height, len_ref, q_ref, k_ref, v_ref, eq_ref, ek_ref, ctx_ref, att_ref):
    seq_len = k_ref.shape[0]
    length = len_ref[0]
    scale = 1.0 / math.sqrt(3 * HEAD_DIM)
    masks = half_masks()
    key_valid = lax.broadcasted_iota(jnp.int32, (1, seq_len), 1) < length
    rows = at * height + lax.broadcasted_iota(jnp.int32, (height, 1), 0)
    rows = jnp.concatenate([rows, rows], axis=0)
    query_valid = rows < length
    row_start = seq_len - height - height * at
    @pl.loop(0, q_ref.shape[1] // LANES)
    def _(pair):
        cols = pl.ds(pl.multiple_of(pair * LANES, LANES), LANES)
        q_pair = q_ref[at * height : (at + 1) * height, cols]
        k_pair = k_ref[:, cols]
        v_pair = v_ref[:, cols]
        rel_window = ek_ref[row_start : row_start + seq_len + height, cols]
        q_two = apart(masks, q_pair)
        content = dot_nt(q_two, k_pair)
        picked = skewed(dot_nt(q_two, rel_window), seq_len + 1)[:, :seq_len]
        blocks = []
        for block in range(seq_len // LANES):
            start = seq_len - LANES - LANES * block + height * at
            window = eq_ref[start : start + LANES + height, cols]
            k_two = apart(masks, k_pair[block * LANES : (block + 1) * LANES])
            tall = skewed(dot_nt(k_two, window), height + 1)[:, :height]
            blocks.append(jnp.concatenate([tall[:LANES].T, tall[LANES:].T], axis=0))
        flipped = jnp.concatenate(blocks, axis=1)
        scores = jnp.where(key_valid, scale * (content + picked + flipped), MASKED)
        peak = jnp.max(scores, axis=-1, keepdims=True)
        weight = jnp.exp(scores - peak)
        total = jnp.sum(weight, axis=-1, keepdims=True)
        keep = jnp.where(query_valid, 1.0 / total, 0.0)
        attend = (weight * keep).astype(BF16)
        att_ref[2 * pair] = attend[:height]
        att_ref[2 * pair + 1] = attend[height:]
        ctx_ref[:, cols] = join(masks, dot_nn(attend, v_pair)).astype(BF16).astype(F32)


def attend(line, at, height, lengths, q, k, v, eq, ek):
    seq_len, cols = q.shape
    heads = cols // HEAD_DIM
    outs = [sds((height, cols), F32), sds((heads, height, seq_len), BF16)]
    return line.call(
        functools.partial(attend_kernel, at, height), f"attend_{at}", outs,
        (lengths, q, k, v, eq, ek), scalars=1,
    )


def norm_back_kernel(
    start, dn_own_ref, dn_other_ref, d_two_ref, xhat_ref, rstd_ref, gain_ref, wout_ref,
    d_one_ref, d_mixed_ref, d_ctx_ref, vec_ref,
):
    rows = slice(start, start + dn_own_ref.shape[0])
    d_normed = (dn_own_ref[...] + dn_other_ref[...]) + d_two_ref[rows]
    xhat = xhat_ref[rows]
    vec_ref[0:1, :] = jnp.sum(d_normed * xhat, axis=0, keepdims=True)
    vec_ref[1:2, :] = jnp.sum(d_normed, axis=0, keepdims=True)
    scaled = d_normed * gain_ref[...].astype(F32)[None, :]
    mean_a = jnp.mean(scaled, axis=-1, keepdims=True)
    mean_b = jnp.mean(scaled * xhat, axis=-1, keepdims=True)
    d_one = rstd_ref[rows] * (scaled - mean_a - xhat * mean_b)
    d_one_ref[...] = d_one
    vec_ref[2:3, :] = jnp.sum(d_one, axis=0, keepdims=True)
    d_mixed = d_one.astype(BF16)
    d_mixed_ref[...] = d_mixed
    d_ctx_ref[...] = dot_nt(d_mixed, wout_ref[...]).astype(BF16)


def norm_back(line, at, start, dn_own, dn_other, d_two, xhat, rstd, gain, wout):
    height, width = dn_own.shape
    outs = [
        sds((height, width), F32),
        sds((height, width), BF16),
        sds((height, wout.shape[0]), BF16),
        sds((8, width), F32),
    ]
    operands = (dn_own, dn_other, d_two, xhat, rstd, gain, wout)
    return line.call(
        functools.partial(norm_back_kernel, start), f"norm_back_{at}", outs, operands,
        flops=BACK_FLOPS,
    )


def attend_back_kernel(
    at, height, count, first, last, d_ctx_ref, q_ref, k_ref, v_ref, eq_ref, ek_ref, *refs
):
    att_refs, refs = refs[:count], refs[count:]
    if not first:
        refs = refs[4:]
    dq_ref, dk_ref, dv_ref, deq_ref, dek_ref = refs[:5]
    seq_len = k_ref.shape[0]
    scale = 1.0 / math.sqrt(3 * HEAD_DIM)
    masks = half_masks()

    def anti(size):
        row = lax.broadcasted_iota(jnp.int32, (size, size), 0)
        col = lax.broadcasted_iota(jnp.int32, (size, size), 1)
        return jnp.where(row + col == size - 1, 1.0, 0.0).astype(BF16)

    anti_rows = anti(height)
    anti_keys = anti(LANES)
    row_start = seq_len - height - height * at
    if first:
        dk_ref[...] = jnp.zeros_like(dk_ref)
        dv_ref[...] = jnp.zeros_like(dv_ref)
        deq_ref[...] = jnp.zeros_like(deq_ref)
        dek_ref[...] = jnp.zeros_like(dek_ref)

    @pl.loop(0, q_ref.shape[1] // LANES)
    def _(pair):
        cols = pl.ds(pl.multiple_of(pair * LANES, LANES), LANES)
        q_pair = q_ref[at * height : (at + 1) * height, cols]
        k_pair = k_ref[:, cols]
        v_pair = v_ref[:, cols]
        ctx_pair = d_ctx_ref[:, cols]
        rel_window = ek_ref[row_start : row_start + seq_len + height, cols]
        q_turned = dot_nn(anti_rows, q_pair).astype(BF16)
        weight = jnp.concatenate(
            [jnp.concatenate([ref[2 * pair + side] for ref in att_refs], axis=0) for side in range(2)],
            axis=0,
        )
        d_att = dot_nt(apart(masks, ctx_pair), v_pair)
        soft = weight.astype(F32)
        inner = jnp.sum(d_att * soft, axis=-1, keepdims=True)
        d_scores = (soft * (d_att - inner)).astype(BF16)
        sides = [d_scores[:height], d_scores[height:]]
        weight_wide = jnp.concatenate([weight[:height], weight[height:]], axis=1)
        dv_ref[:, cols] += join(masks, dot_tn(weight_wide, ctx_pair))
        d_q = join(masks, dot_nn(d_scores, k_pair))
        d_scores_t = [side.T for side in sides]
        d_k = join(masks, dot_nn(jnp.concatenate(d_scores_t, axis=0), q_pair))
        turned = dot_nn(anti_rows, jnp.concatenate(sides, axis=1))
        space = jnp.zeros((height, height), F32)
        turned = [
            jnp.concatenate([turned[:, side * seq_len : (side + 1) * seq_len], space], axis=1)
            for side in range(2)
        ]
        turned = skewed(jnp.concatenate(turned, axis=0), 0).astype(BF16)
        d_q_turned = join(masks, dot_nn(turned, rel_window))
        turned_wide = jnp.concatenate([turned[:height], turned[height:]], axis=1)
        d_rel_k = join(masks, dot_tn(turned_wide, q_turned))
        dek_ref[row_start : row_start + seq_len + height, cols] += scale * d_rel_k

        def turn_back(matrix, value):
            high = value.astype(BF16)
            rest = (value - high.astype(F32)).astype(BF16)
            both = dot_nn(matrix, jnp.concatenate([high, rest], axis=1))
            return both[:, :LANES] + both[:, LANES:]

        dq_ref[:, cols] = (scale * (d_q + turn_back(anti_rows, d_q_turned))).astype(BF16)
        backs = []
        for block in range(seq_len // LANES):
            start = seq_len - LANES - LANES * block + height * at
            rows = slice(block * LANES, (block + 1) * LANES)
            window = eq_ref[start : start + LANES + height, cols]
            tall = dot_nn(anti_keys, jnp.concatenate([side[rows] for side in d_scores_t], axis=1))
            space = jnp.zeros((LANES, LANES), F32)
            tall = [
                jnp.concatenate([tall[:, side * height : (side + 1) * height], space], axis=1)
                for side in range(2)
            ]
            tall = skewed(jnp.concatenate(tall, axis=0), 0).astype(BF16)
            backs.append(join(masks, dot_nn(tall, window)))
            k_turned = apart(masks, dot_nn(anti_keys, k_pair[rows]).astype(BF16))
            deq_ref[start : start + LANES + height, cols] += scale * dot_tn(tall, k_turned)
        for block, value in enumerate(backs):
            rows = slice(block * LANES, (block + 1) * LANES)
            dk_ref[rows, cols] += scale * (d_k[rows] + turn_back(anti_keys, value))
    if last:
        dk_low_ref, dv_low_ref = refs[5:]
        dk_low_ref[...] = dk_ref[...].astype(BF16)
        dv_low_ref[...] = dv_ref[...].astype(BF16)


def attend_back(line, at, height, last, d_ctx, q, k, v, eq, ek, att, carried):
    seq_len, cols = q.shape
    operands = [d_ctx, q, k, v, eq, ek, *att, *carried]
    outs = [
        sds((height, cols), BF16),
        sds((seq_len, cols), F32),
        sds((seq_len, cols), F32),
        sds((2 * seq_len, cols), F32),
        sds((2 * seq_len, cols), F32),
    ]
    if last:
        outs += [sds((seq_len, cols), BF16)] * 2
    base = 6 + len(att)
    return line.call(
        functools.partial(attend_back_kernel, at, height, len(att), not carried, last),
        f"attend_back_{at}", outs, operands,
        aliases={base + place: 1 + place for place in range(4)} if carried else {},
        flops=BACK_FLOPS,
    )


def feed_kernel(
    at, height, count, wout_ref, bout_ref, hidden_ref, gain_ref, shift_ref, win_ref, bin_ref,
    wdown_ref, *refs,
):
    own_refs, other_refs = refs[:count], refs[count : 2 * count]
    xhat_ref, rstd_ref, normed_ref, act_ref, slope_ref, low_ref = refs[2 * count :]
    own = jnp.concatenate([ref[...] for ref in own_refs], axis=0)
    other = jnp.concatenate([ref[...] for ref in other_refs], axis=0)
    first = lax.axis_index("head") == 0
    ctx = jnp.concatenate([jnp.where(first, own, other), jnp.where(first, other, own)], axis=1)
    ctx = ctx.astype(BF16)
    mixed = dot_nn(ctx, wout_ref[...])
    hidden = hidden_ref[at * height : (at + 1) * height].astype(F32)
    resid = mixed + bout_ref[...].astype(F32)[None, :] + hidden
    center = resid - jnp.mean(resid, axis=-1, keepdims=True)
    spread = jnp.mean(center * center, axis=-1, keepdims=True)
    rstd = lax.rsqrt(spread + EPSILON)
    xhat = center * rstd
    xhat_ref[...] = xhat
    rstd_ref[...] = rstd
    normed = xhat * gain_ref[...].astype(F32)[None, :] + shift_ref[...].astype(F32)[None, :]
    low = normed.astype(BF16)
    normed_ref[...] = low
    units = win_ref.shape[1]
    step = units // 3
    total = None
    bias = bin_ref[...].astype(F32)[None, :]
    for part in range(3):
        cols = slice(part * step, (part + 1) * step)
        inner = dot_nn(low, win_ref[:, cols]) + bias[:, cols]
        phi = 0.5 * (1.0 + lax.erf(inner * math.sqrt(0.5)))
        act = (inner * phi).astype(BF16)
        slope = phi + inner * (jnp.exp(-0.5 * inner * inner) * (1.0 / math.sqrt(2 * math.pi)))
        act_ref[:, cols] = act
        slope_ref[:, cols] = slope
        term = dot_nn(act, wdown_ref[cols, :])
        total = term if total is None else total + term
    low_ref[...] = total


def feed(line, at, height, own, other, wout, bout, hidden, gain, shift, win, b_in, wdown):
    width = hidden.shape[1]
    units = win.shape[1]
    outs = [
        sds((height, width), F32),
        sds((height, 1), F32),
        sds((height, width), BF16),
        sds((height, units), BF16),
        sds((height, units), F32),
        sds((height, width), F32),
    ]
    operands = (wout, bout, hidden, gain, shift, win, b_in, wdown, *own, *other)
    return line.call(
        functools.partial(feed_kernel, at, height, len(own)), f"feed_{at}", outs, operands,
        flops=BACK_FLOPS if at else 1024,
    )


def feed_back_kernel(
    at, height, count, low_own_ref, low_other_ref, xhat_one_ref, gain_one_ref, shift_one_ref, bdown_ref,
    gain_ref, shift_ref, cot_ref, slope_ref, win_ref, wdown_ref,
    *refs,
):
    before, refs = refs[:count], refs[count:]
    out_ref, d_two_ref, d_low_ref, d_inner_ref, vec_ref, bin_ref, *dn_refs = refs
    normed = xhat_one_ref[...] * gain_one_ref[...].astype(F32)[None, :]
    normed = normed + shift_one_ref[...].astype(F32)[None, :]
    resid = (low_own_ref[...] + low_other_ref[...]) + bdown_ref[...].astype(F32)[None, :] + normed
    center = resid - jnp.mean(resid, axis=-1, keepdims=True)
    spread = jnp.mean(center * center, axis=-1, keepdims=True)
    rstd = lax.rsqrt(spread + EPSILON)
    xhat = center * rstd
    gain = gain_ref[...].astype(F32)[None, :]
    value = (xhat * gain + shift_ref[...].astype(F32)[None, :]).astype(BF16)
    if out_ref.shape[0] == height:
        out_ref[...] = value
    else:
        for stream, ref in enumerate(before):
            out_ref[stream * height : (stream + 1) * height] = ref[...]
        out_ref[at * height : (at + 1) * height] = value
    err = cot_ref[at * height : (at + 1) * height].astype(F32)
    vec_ref[0:1, :] = jnp.sum(err * xhat, axis=0, keepdims=True)
    vec_ref[1:2, :] = jnp.sum(err, axis=0, keepdims=True)
    scaled = err * gain
    mean_a = jnp.mean(scaled, axis=-1, keepdims=True)
    mean_b = jnp.mean(scaled * xhat, axis=-1, keepdims=True)
    d_two = rstd * (scaled - mean_a - xhat * mean_b)
    d_two_ref[...] = d_two
    vec_ref[2:3, :] = jnp.sum(d_two, axis=0, keepdims=True)
    low = d_two.astype(BF16)
    d_low_ref[...] = low
    units = win_ref.shape[1]
    step = units // 3
    total = None
    for part in range(3):
        cols = slice(part * step, (part + 1) * step)
        d_act = dot_nt(low, wdown_ref[cols, :])
        d_inner = (d_act * slope_ref[:, cols]).astype(BF16)
        d_inner_ref[:, cols] = d_inner
        bin_ref[0:1, cols] = jnp.sum(d_inner.astype(F32), axis=0, keepdims=True)
        term = dot_nt(d_inner, win_ref[:, cols])
        total = term if total is None else total + term
    rows = dn_refs[0].shape[0]
    for piece, ref in enumerate(dn_refs):
        ref[...] = total[piece * rows : (piece + 1) * rows]


def feed_back(
    line, at, height, rows, before, low_own, low_other, xhat, gain_one, shift_one, bdown, gain,
    shift, cot, slope, win, wdown,
):
    width = cot.shape[1]
    units = win.shape[1]
    last = (at + 1) * height == cot.shape[0]
    before = before if last else []
    outs = [
        sds(cot.shape if last else (height, width), BF16),
        sds((height, width), F32),
        sds((height, width), BF16),
        sds((height, units), BF16),
        sds((8, width), F32),
        sds((8, units), F32),
    ]
    outs += [sds((rows, width), F32)] * (height // rows)
    operands = (
        low_own, low_other, xhat, gain_one, shift_one, bdown, gain, shift, cot, slope, win, wdown,
        *before,
    )
    return line.call(
        functools.partial(feed_back_kernel, at, height, len(before)), f"feed_back_{at}", outs,
        operands, direct=(0,) if last else (),
    )


def spread(order, me, total, kept_ref, sent_refs, cols):
    parts = 1 << len(order)
    height = total.shape[0] // parts
    for bit in (0, order[0]):

        @pl.when((me & order[0]) == bit)
        def _(bit=bit):
            for block in range(parts):
                origin = me ^ block
                place = 0
                for later in order[1:]:
                    place = 2 * place + ((origin >> (later.bit_length() - 1)) & 1)
                top = block * height
                if block & order[0] == bit:
                    kept_ref[place, :, cols] = total[top : top + height]
                else:
                    for ref in sent_refs:
                        ref[place, :, cols] = total[top : top + ref.shape[1]]
                        top += ref.shape[1]


def grad_kernel(order, groups, pieces, *refs):
    kept_ref, *sent_refs = refs[-1 - pieces :]
    me = lax.axis_index("dp")
    at, start = 0, 0
    for count in groups:
        terms = []
        for rights in count:
            terms.append((refs[at], refs[at + 1 : at + 1 + rights]))
            at += 1 + rights
        width = terms[0][1][0].shape[1]

        def part(index, terms=terms, start=start):
            total = None
            columns = pl.ds(pl.multiple_of(index * COLUMNS, COLUMNS), COLUMNS)
            for left_ref, right_refs in terms:
                right = jnp.concatenate([ref[:, columns] for ref in right_refs], axis=0)
                term = dot_tn(left_ref[...], right.astype(BF16))
                total = term if total is None else total + term
            target = pl.ds(pl.multiple_of(start + index * COLUMNS, COLUMNS), COLUMNS)
            spread(order, me, total, kept_ref, sent_refs, target)

        pl.loop(0, width // COLUMNS)(part)
        start += width


def halves(order, rows, cols, pieces):
    half, height = (1 << len(order)) // 2, rows >> len(order)
    return [sds((half, height, cols), F32)] + [sds((half, height // pieces, cols), F32)] * pieces


def grad_blocks(line, name, order, groups, pieces=1):
    width = groups[0][0][0].shape[1]
    cols = sum(group[0][1][0].shape[1] for group in groups)
    operands = [array for group in groups for left, right in group for array in (left, *right)]
    counts = [[len(right) for _, right in group] for group in groups]
    outs = halves(order, width, cols, pieces)
    return line.call(
        functools.partial(grad_kernel, order, counts, pieces), name, outs, operands,
        flops=GRAD_FLOPS,
    )


def rel_kernel(
    order, counts, table_rows, bucket_ref, deq_ref, dek_ref, wq_ref, wk_ref, dk_ref, dv_ref,
    *refs,
):
    groups = []
    for count in counts:
        groups.append(refs[:count])
        refs = refs[count:]
    dq_refs, one_refs, two_refs, unit_refs = groups
    relq_ref, relk_ref, kept_ref, *sent_refs, pack_ref = refs
    onehot = onehot_of(bucket_ref, table_rows)
    deq, dek = deq_ref[...], dek_ref[...]
    cols = deq.shape[1]
    d_rel = dot_nn(onehot, jnp.concatenate([deq, dek], axis=1).astype(BF16)).astype(BF16)
    relq_ref[...] = d_rel[:, :cols]
    relk_ref[...] = d_rel[:, cols:]
    total = dot_nt(d_rel, jnp.concatenate([wq_ref[...], wk_ref[...]], axis=1))
    width = total.shape[1]
    me = lax.axis_index("dp")
    spread(order, me, total, kept_ref, sent_refs, slice(0, width))

    def summed(value):
        return jnp.sum(value.astype(F32), axis=0, keepdims=True)

    def over(stream_refs):
        value = stream_refs[0][...]
        for ref in stream_refs[1:]:
            value = value + ref[...]
        return value

    one, two, unit = over(one_refs), over(two_refs), over(unit_refs)
    d_bias = summed(dq_refs[0][...])
    for ref in dq_refs[1:]:
        d_bias = d_bias + summed(ref[...])
    vectors = [
        d_bias + summed(deq),
        summed(dk_ref[...]) + summed(dek),
        summed(dv_ref[...]),
        one[2:3], one[0:1], one[1:2], unit[0:1], two[2:3], two[0:1], two[1:2],
    ]
    pack_ref[...] = jnp.zeros_like(pack_ref)
    row = 0
    for vector in vectors:
        for piece in range(vector.shape[1] // LANES):
            pack_ref[row : row + 1, :] = vector[:, piece * LANES : (piece + 1) * LANES]
            row += 1
    spread(order, me, pack_ref[...], kept_ref, sent_refs, slice(width, width + LANES))


def rel_grads(line, order, span, buckets, deq, dek, wq, wk, dk, dv, dq, one, two, unit):
    width, cols = wq.shape
    outs = [sds((span, cols), BF16)] * 2
    outs = outs + halves(order, span, width + LANES, REL_PIECES)
    operands = [buckets, deq, dek, wq, wk, dk, dv, *dq, *one, *two, *unit]
    return line.call(
        functools.partial(rel_kernel, order, [len(g) for g in (dq, one, two, unit)], span), "rel_grads", outs, operands,
        scratch=[pltpu.VMEM((span, LANES), F32)],
    )


def rel_split_kernel(own_ref, other_ref, table_ref, vector_ref):
    width = table_ref.shape[2]
    for at in range(2):
        total = own_ref[at] + other_ref[1 - at]
        table_ref[at] = total[:, :width]
        vector_ref[at] = total[:, width:]


def rel_split(own, other):
    count, rows, wide = own.shape
    outs = [sds((count, rows, wide - LANES), F32), sds((count, rows, LANES), F32)]
    return rel_split_kernel, "rel_split", outs, [own, other], ()


def rel_join_kernel(own_ref, other_ref, vector_ref, out_ref):
    width = own_ref.shape[2]
    out_ref[:, :, :width] = own_ref[...] + other_ref[...]
    out_ref[:, :, width:] = vector_ref[...]


def rel_join(own, other, vector):
    count, rows, width = own.shape
    outs = [sds((count, rows, width + vector.shape[2]), F32)]
    return rel_join_kernel, "rel_join", outs, [own, other, vector], ()


def hidden_join_kernel(own_ref, other_ref, *refs):
    out_ref = refs[-1]
    start = 0
    for ref in refs[:-1]:
        rows = slice(start, start + ref.shape[0])
        out_ref[rows] = ((own_ref[rows] + other_ref[rows]) + ref[...]).astype(BF16)
        start += ref.shape[0]


def hidden_join(own, other, d_one):
    outs = [sds(own.shape, BF16)]
    return hidden_join_kernel, "hidden_join", outs, [own, other, *d_one], (0,)


def unpack_kernel(origins, count, *refs):
    shared_refs, (table_ref, *vector_refs) = refs[:count], refs[count:]
    width = table_ref.shape[2]
    height = table_ref.shape[1]
    me = lax.axis_index("dp")
    places = [(ref, at) for ref in shared_refs for at in range(ref.shape[0])]
    rows = sum(ref.shape[0] for ref in vector_refs) // LANES
    lines = [
        (ref, piece) for ref in vector_refs for piece in range(ref.shape[0] // LANES)
    ]
    for (shared_ref, at), origin in zip(places, origins, strict=True):
        table_ref[me ^ origin] = shared_ref[at, :, :width]
        for block in range((rows + height - 1) // height):

            @pl.when(me ^ origin == block)
            def _(shared_ref=shared_ref, at=at, block=block):
                for row in range(block * height, min(rows, (block + 1) * height)):
                    ref, piece = lines[row]
                    inner = row % height
                    line = shared_ref[at, inner : inner + 1, width:]
                    ref[pl.ds(piece * LANES, LANES)] = line.reshape(LANES)


def unpack(origins, pieces, sizes):
    height, wide = pieces[0].shape[1:]
    outs = [sds((len(origins), height, wide - LANES), F32)] + [sds((size,), F32) for size in sizes]
    kernel = functools.partial(unpack_kernel, origins, len(pieces))
    return kernel, "unpack", outs, list(pieces), range(len(outs))


def hidden_kernel(dk_ref, dv_ref, wq_ref, wk_ref, wv_ref, *refs):
    out_ref = refs[-1]
    out_ref[...] = dot_nt(dk_ref[...], wk_ref[...]) + dot_nt(dv_ref[...], wv_ref[...])
    start = 0
    for ref in refs[:-1]:
        out_ref[start : start + ref.shape[0]] += dot_nt(ref[...], wq_ref[...])
        start += ref.shape[0]


def hidden_grad(line, dk, dv, wq, wk, wv, dq):
    out = sds((dk.shape[0], wq.shape[0]), F32)
    (total,) = line.call(
        hidden_kernel, "hidden_grad", [out], (dk, dv, wq, wk, wv, *dq)
    )
    return total


def bits_of(parts):
    return [1 << b for b in range(parts.bit_length() - 1)]


def swap_head(value):
    return lax.ppermute(value, "head", [(0, 1), (1, 0)])


def flip(value, parts, bit):
    return lax.ppermute(value, "dp", [(i, i ^ bit) for i in range(parts)])


def together(*values):
    return lax.optimization_barrier(values)


def step_kernel(kept_ref, *refs):
    *arrived_refs, kept_out, sent_out = refs
    half = kept_out.shape[0]
    top = 0
    for ref in arrived_refs:
        rows = slice(top, top + ref.shape[1])
        kept_out[:, rows] = kept_ref[:half, rows] + ref[:half]
        sent_out[:, rows] = kept_ref[half:, rows] + ref[half:]
        top += ref.shape[1]


class Scatter:
    def __init__(self, line, name, kept, *sent, order):
        self.line, self.name, self.order = line, name, list(order)
        self.parts = 1 << len(self.order)
        self.kept = kept
        self.send(sent)

    def send(self, sent):
        self.bit = self.order.pop(0)
        self.arrived = [flip(piece, self.parts, self.bit) for piece in sent]

    def step(self):
        shape = (self.kept.shape[0] // 2, *self.kept.shape[1:])
        self.kept, sent = yield (
            step_kernel, f"{self.name}_{self.bit}", [sds(shape, F32)] * 2,
            [self.kept, *self.arrived], (),
        )
        self.send([sent])

    def rest(self, left=0):
        while len(self.order) > left:
            self.line.group([self.step()])

    def exchange(self):
        def add(kept_ref, arrived_ref, out_ref):
            out_ref[...] = kept_ref[...] + arrived_ref[...]

        self.rest(1)
        outs = [sds(self.kept.shape, F32)]
        (self.both,) = yield add, f"{self.name}_{self.bit}", outs, [self.kept, *self.arrived], ()
        bit = self.order.pop(0)
        self.both_other, self.origins = flip(self.both, self.parts, bit), [0, bit]

    def finish(self, widths):
        def kernel(kept_ref, arrived_ref, *out_refs):
            start = 0
            for ref in out_refs:
                cols = slice(start, start + ref.shape[1])
                ref[...] = kept_ref[0, :, cols] + arrived_ref[0, :, cols]
                start += ref.shape[1]

        self.rest()
        outs = [sds((self.kept.shape[1], width), F32) for width in widths]
        operands = [self.kept, *self.arrived]
        self.sums = yield kernel, f"{self.name}_sum", outs, operands, range(len(outs))


def pack_kernel(*refs):
    start = 0
    for ref in refs[:-1]:
        refs[-1][start : start + ref.shape[0]] = ref[...]
        start += ref.shape[0]


class Gather:
    def __init__(self, line, value, origins, parts, order):
        self.line, self.parts, self.order = line, parts, list(order)
        self.pieces, self.origins = [value], origins
        self.send(value)

    def send(self, sent):
        bit = self.order.pop(0)
        self.pieces.append(flip(sent, self.parts, bit))
        self.origins = self.origins + [origin ^ bit for origin in self.origins]

    def step(self):
        shape = (len(self.origins), *self.pieces[0].shape[1:])
        name = f"pack_{len(self.origins)}"
        (sent,) = yield pack_kernel, name, [sds(shape, F32)], list(self.pieces), ()
        self.send(sent)

    def rest(self):
        while self.order:
            self.line.group([self.step()])


def words_of(text):
    words, open_word = [], None
    for letter in text:
        if letter == "(":
            open_word = ""
        elif letter == ")":
            words.append(open_word)
            open_word = None
        elif open_word is not None:
            open_word += letter
        else:
            words.append(letter)
    return words


def on_device(parts, *arguments):
    (
        hidden_in, lengths, cotangent, w_query, b_query, w_key, b_key, w_value, b_value,
        w_out, b_out, ln1_gain, ln1_bias, w_in, b_in, w_down, b_down, ln2_gain, ln2_bias,
        rel_table,
    ) = arguments
    seq_len, width = hidden_in.shape
    height = seq_len // STREAMS
    streams = range(STREAMS)
    bits = bits_of(parts)

    buckets = jnp.asarray(distance_buckets(seq_len)[None, :])
    line = Line()
    q, k, v, eq, ek, mine = project(
        line, buckets, hidden_in, w_query, b_query, w_key, b_key, w_value, b_value, rel_table,
        w_out,
    )
    fetched = swap_head(mine)
    contexts, attends = [], []
    for at in range(CONTEXTS * STREAMS):
        context, attended = attend(line, at, height // CONTEXTS, lengths, q, k, v, eq, ek)
        contexts.append(context)
        attends.append(attended)
    fetched, contexts[0] = together(fetched, contexts[0])
    quarters = [fetched, flip(fetched, parts, 1), flip(fetched, parts, 2)]
    quarters.append(flip(quarters[2], parts, 1))
    w_out_all = assemble(line, w_out, quarters)
    others = [swap_head(context) for context in contexts]
    of_stream = [slice(CONTEXTS * at, CONTEXTS * (at + 1)) for at in streams]
    fed = [
        feed(
            line, at, height, contexts[of_stream[at]], others[of_stream[at]],
            w_out_all, b_out, hidden_in, ln1_gain, ln1_bias, w_in, b_in, w_down,
        )
        for at in streams
    ]
    backs = []
    for at in streams:
        xhat, rstd, normed, act, slope, lowered = fed[at]
        backs.append(
            feed_back(
                line, at, height, height, [b[0] for b in backs], lowered, swap_head(lowered), xhat,
                ln1_gain, ln1_bias, b_down, ln2_gain, ln2_bias, cotangent, slope, w_in, w_down,
            )
        )
    output = backs[-1][0]
    crossed = bits[:1] + bits[2:] + bits[1:2]
    g_down = grad_blocks(
        line, "grad_down", bits, [[(backs[at][2], fed[at][3:4]) for at in streams]]
    )
    down = Scatter(line, "down", *g_down, order=bits)
    g_in = grad_blocks(
        line, "grad_in", crossed, [[(fed[at][2], backs[at][3:4]) for at in streams]]
    )
    inner = Scatter(line, "inner", *g_in, order=crossed)
    norms, dq = [], []
    carried = ()
    for at in streams:
        xhat, rstd = fed[at][:2]
        d_two, dn = backs[at][1], backs[at][6]
        norms.append(
            norm_back(line, at, 0, dn, swap_head(dn), d_two, xhat, rstd, ln1_gain, w_out)
        )
        if at == 0:
            line.group([down.step()])
            line.group([inner.step()])
        d_q, *carried = attend_back(
            line, at, height, at == streams[-1], norms[at][2], q, k, v, eq, ek,
            attends[of_stream[at]], carried,
        )
        dq.append(d_q)
    deq, dek, dk, dv = carried[2:]
    cols = q.shape[1]
    hidden_parts = [hidden_in[at * height : (at + 1) * height] for at in streams]
    chains = {"d": down, "i": inner}
    made = {}

    def start_rel():
        made["relq"], made["relk"], *blocks = rel_grads(
            line, bits, rel_table.shape[0], buckets, deq, dek, w_query, w_key, dk, dv, dq,
            [n[3] for n in norms], [b[4] for b in backs], [b[5] for b in backs],
        )
        chains["r"] = Scatter(line, "rel", *blocks, order=bits)

    def start_value_out():
        blocks = grad_blocks(
            line, "grad_value_out", bits,
            [
                [(hidden_in, [dv])],
                [(norms[at][1], contexts[of_stream[at]]) for at in streams],
            ],
            HEAD_PIECES,
        )
        chains["v"] = Scatter(line, "value_out", *blocks, order=bits)

    def start_query_key():
        blocks = grad_blocks(
            line, "grad_query_key", bits,
            [
                [*zip(hidden_parts, [[d] for d in dq], strict=True), (rel_table, [made["relq"]])],
                [(hidden_in, [dk]), (rel_table, [made["relk"]])],
            ],
            HEAD_PIECES,
        )
        chains["q"] = Scatter(line, "query_key", *blocks, order=bits)

    def start_hidden():
        made["hidden"] = hidden_grad(line, dk, dv, w_query, w_key, w_value, dq)
        made["hidden_other"] = swap_head(made["hidden"])

    def swap_rel():
        both, other = chains["r"].both, chains["r"].both_other
        made["own"], made["vectors"] = yield rel_split(both, other)
        made["own_other"] = swap_head(made["own"])

    def gather_rel():
        (joined,) = yield rel_join(made["own"], made["own_other"], made["vectors"])
        chains["p"] = Gather(line, joined, chains["r"].origins, parts, bits[-2::-1])

    def end_hidden():
        d_one = [n[0] for n in norms]
        made["grad_input"] = yield hidden_join(made["hidden"], made["hidden_other"], d_one)

    def end_rel():
        chains["p"].rest()
        sizes = [cols] * 3 + [width] * 3 + [w_in.shape[1]] + [width] * 3
        made["shared"] = yield unpack(chains["p"].origins, chains["p"].pieces, sizes)

    starters = {
        "L": start_rel, "G": start_value_out, "K": start_query_key, "Y": start_hidden,
    }
    steps = {
        "X": lambda: chains["r"].exchange(), "S": swap_rel, "J": gather_rel, "H": end_hidden,
        "U": end_rel,
    }
    widths = {"d": [w_in.shape[1]], "i": [w_in.shape[1]], "v": [cols, cols], "q": [cols, cols]}

    def work(letter):
        if letter in widths:
            return chains[letter].finish(widths[letter])
        return steps[letter]() if letter in steps else chains[letter.lower()].step()

    for word in words_of(TAIL):
        if word in starters:
            starters[word]()
        else:
            line.group([work(letter) for letter in word])
    (s_down,), (s_in,) = chains["d"].sums, chains["i"].sums
    (s_q, s_k), (s_v, s_out) = chains["q"].sums, chains["v"].sums
    (grad_input,) = made["grad_input"]
    table_blocks, *pieces = made["shared"]
    grad_rel_table = table_blocks.reshape(rel_table.shape)
    (
        grad_b_query, grad_b_key, grad_b_value, grad_b_out, grad_ln1_gain, grad_ln1_bias,
        grad_b_in, grad_b_down, grad_ln2_gain, grad_ln2_bias,
    ) = pieces
    return (
        output, grad_input, s_q, grad_b_query, s_k, grad_b_key, s_v, grad_b_value,
        s_out.T, grad_b_out, grad_ln1_gain, grad_ln1_bias, s_in, grad_b_in,
        s_down.T, grad_b_down, grad_ln2_gain, grad_ln2_bias, grad_rel_table,
    )


def solution(mesh):
    parts = mesh.shape["dp"]
    return jax.shard_map(
        functools.partial(on_device, parts),
        mesh=mesh,
        in_specs=(
            P("dp", None), P("dp"), P("dp", None),
            P(None, "head"), P("head"), P(None, "head"), P("head"), P(None, "head"), P("head"),
            P("head", None), P(), P(), P(),
            P(None, "head"), P("head"), P("head", None), P(), P(), P(), P(),
        ),
        out_specs=(
            P("dp", None), P("dp", None),
            P("dp", "head"), P("head"), P("dp", "head"), P("head"), P("dp", "head"), P("head"),
            P("head", "dp"), P(), P(), P(),
            P("dp", "head"), P("head"), P("head", "dp"), P(), P(), P(), P(),
        ),
        check_vma=False,
    )
```

profile of v0, /device:TPU:0, one launch (start us, length us, event | category | flops | bytes accessed | tf_op | source)
XLA Modules:
  0.0 216.3 jit_solution(8293450671349664434)
XLA Ops:
  0.7 5.0 %project.1 = (bf16[512,384]{1,0:T(8,128)(2,1)S(1)}, bf16[512,384]{1,0:T(8,128)(2,1)S(1)}, bf16[512,384]{1,0:T(8,128)(2,1)S(1)}, bf16[1024,384]{1,0:T(8,128)(2,1)...) custom-call(s32[1,1024]{1,0:T(1,128)} %constant.2.clone.refs_0_, bf16[512,768]{1,0:T(8,128)(2,1)} %refs_0_.7, ...), custom_call_target="tpu_custom_call" | custom-call | flops 1024 | bytes 1024 | tf_op jit(solution)/shard_map/project/pallas_call | solution.py:87
  5.7 3.0 %collective-permute-start = (f32[96,768]{1,0:T(8,128)S(1)}, f32[96,768]{1,0:T(8,128)S(1)}, u32[]{:S(2)}, u32[]{:S(2)}) collective-permute-start(f32[96,768]{1,0:T(8,128)S(1)} %get-tuple-element.133.refs_6_), channel_id=1, source_target_pairs={{0,1},{1,0},{2,3},{3,2},{4,5},{5,4},{6,7},{7,6},{8,9},{9,8},{10,11... | collective-permute-start | bytes 884744 | tf_op jit(solution)/shard_map/ppermute | solution.py:782
  9.4 7.0 %attend_0.1 = (f32[256,384]{1,0:T(8,128)S(1)}, bf16[6,256,512]{2,1,0:T(8,128)(2,1)S(1)}) custom-call(s32[1]{0:T(128)S(6)} %copy.48.refs_0_, bf16[512,384]{1,0:T(8,128)(2,1)S(1)} %get-tuple-element.134.refs_1_, bf16[512,384]{1,0:T(8,128)(2,1)S(1)} %get-tuple-element.135.refs_2_, bf16[512,384]{1,0:T(8,128)(2,1)S(1)} %get-tuple-element.136.refs_3_, ...), custom_call_target="tpu_custom_call" | custom-call | flops 1024 | bytes 1024 | tf_op jit(solution)/shard_map/attend_0/pallas_call | solution.py:87
  19.0 7.2 %attend_1.1 = (f32[256,384]{1,0:T(8,128)S(1)}, bf16[6,256,512]{2,1,0:T(8,128)(2,1)S(1)}) custom-call(s32[1]{0:T(128)S(6)} %copy.48.refs_0_, bf16[512,384]{1,0:T(8,128)(2,1)S(1)} %get-tuple-element.134.refs_1_, bf16[512,384]{1,0:T(8,128)(2,1)S(1)} %get-tuple-element.135.refs_2_, bf16[512,384]{1,0:T(8,128)(2,1)S(1)} %get-tuple-element.136.refs_3_, ...), custom_call_target="tpu_custom_call" | custom-call | flops 1024 | bytes 1024 | tf_op jit(solution)/shard_map/attend_1/pallas_call | solution.py:87
  29.6 2.8 %feed_0.1 = (f32[256,768]{1,0:T(8,128)S(1)}, f32[256,1]{1,0:T(8,128)S(1)}, bf16[256,768]{1,0:T(8,128)(2,1)S(1)}, bf16[256,1536]{1,0:T(8,128)(2,1)S(1)}, f32[256,1536]{1,0:T(8,128)S(1)}, /*index=5*/f32[256,768]{1,0:T(8,128)S(1)}) custom-call(bf16[768,768]{1,0:T(8,128)(2,1)S(1)} %bitcast.4, bf16[768]{0:T(1024)(128)(2,1)S(1)} %copy-done.43, ...), custom_call_target="tpu_custom_call" | custom-call | flops 1024 | bytes 1024 | tf_op jit(solution)/shard_map/feed_0/pallas_call | solution.py:87
  33.5 4.8 %collective-permute-done.4.refs_9_ = f32[256,384]{1,0:T(8,128)S(1)} collective-permute-done((f32[256,384]{1,0:T(8,128)S(1)}, f32[256,384]{1,0:T(8,128)S(1)}, u32[]{:S(2)}, u32[]{:S(2)}) %collective-permute-start.4) | collective-permute-done | bytes 393248 | tf_op jit(solution)/shard_map/ppermute | solution.py:782
  38.2 2.8 %feed_1.1 = (f32[256,768]{1,0:T(8,128)S(1)}, f32[256,1]{1,0:T(8,128)S(1)}, bf16[256,768]{1,0:T(8,128)(2,1)S(1)}, bf16[256,1536]{1,0:T(8,128)(2,1)S(1)}, f32[256,1536]{1,0:T(8,128)S(1)}, /*index=5*/f32[256,768]{1,0:T(8,128)S(1)}) custom-call(bf16[768,768]{1,0:T(8,128)(2,1)S(1)} %bitcast.5, bf16[768]{0:T(1024)(128)(2,1)S(1)} %copy-done.43, ...), custom_call_target="tpu_custom_call" | custom-call | flops 68719476736 | bytes 1024 | tf_op jit(solution)/shard_map/feed_1/pallas_call | solution.py:87
  41.4 13.6 %collective-permute-done.7.refs_1_ = f32[256,768]{1,0:T(8,128)S(1)} collective-permute-done((f32[256,768]{1,0:T(8,128)S(1)}, f32[256,768]{1,0:T(8,128)S(1)}, u32[]{:S(2)}, u32[]{:S(2)}) %collective-permute-start.7) | collective-permute-done | bytes 786464 | tf_op jit(solution)/shard_map/ppermute | solution.py:782
  57.9 14.0 %collective-permute-done.6.refs_1_ = f32[256,768]{1,0:T(8,128)S(1)} collective-permute-done((f32[256,768]{1,0:T(8,128)S(1)}, f32[256,768]{1,0:T(8,128)S(1)}, u32[]{:S(2)}, u32[]{:S(2)}) %collective-permute-start.6) | collective-permute-done | bytes 786464 | tf_op jit(solution)/shard_map/ppermute | solution.py:782
  71.9 3.1 %feed_back_1.1 = (bf16[512,768]{1,0:T(8,128)(2,1)}, f32[256,768]{1,0:T(8,128)S(1)}, bf16[256,768]{1,0:T(8,128)(2,1)S(1)}, bf16[256,1536]{1,0:T(8,128)(2,1)S(1)},...) custom-call(f32[256,768]{1,0:T(8,128)S(1)} %get-tuple-element.144.refs_0_, ...), custom_call_target="tpu_custom_call" | custom-call | flops 1024 | bytes 1024 | tf_op jit(solution)/shard_map/feed_back_1/pallas_call | solution.py:87
  77.9 3.0 %grad_in.1 = (f32[8,48,1536]{2,1,0:T(8,128)S(1)}, f32[8,48,1536]{2,1,0:T(8,128)S(1)}) custom-call(bf16[256,768]{1,0:T(8,128)(2,1)S(1)} %get-tuple-element.158.refs_0_, bf16[256,1536]{1,0:T(8,128)(2,1)S(1)} %get-tuple-element.159.refs_1_, bf16[256,768]{1,0:T(8,128)(2,1)S(1)} %get-tuple-element.160.refs_2_, bf16[256,1536]{1,0:T(8,128)(2,1)S(1)} %get-tuple-element.161.refs_3_, ...), custom_call_target="tpu_custom_call" | custom-call | flops 1024 | bytes 1024 | tf_op jit(solution)/shard_map/grad_in/pallas_call | solution.py:87
  81.8 7.0 %collective-permute-done.9.refs_1_ = f32[256,768]{1,0:T(8,128)S(1)} collective-permute-done((f32[256,768]{1,0:T(8,128)S(1)}, f32[256,768]{1,0:T(8,128)S(1)}, u32[]{:S(2)}, u32[]{:S(2)}) %collective-permute-start.9) | collective-permute-done | bytes 786464 | tf_op jit(solution)/shard_map/ppermute | solution.py:782
  94.4 9.7 %attend_back_0.1 = (bf16[256,384]{1,0:T(8,128)(2,1)S(1)}, f32[512,384]{1,0:T(8,128)S(1)}, f32[512,384]{1,0:T(8,128)S(1)}, f32[1024,384]{1,0:T(8,128)S(1)}, f32[1024,384]{1,0:T(8,128)S(1)}) custom-call(bf16[256,384]{1,0:T(8,128)(2,1)S(1)} %get-tuple-element.169.refs_0_, bf16[512,384]{1,0:T(8,128)(2,1)S(1)} %copy-done.18, bf16[512,384]{1,0:T(8,128)(2,1)S(1)} %copy-done.20, ...), custom_call_target="tpu_custom_call" | custom-call | flops 68719476736 | bytes 1024 | tf_op jit(solution)/shard_map/attend_back_0/pallas_call | solution.py:87
  105.0 9.5 %attend_back_1.1 = (bf16[256,384]{1,0:T(8,128)(2,1)S(1)}, f32[512,384]{1,0:T(8,128)S(1)}, f32[512,384]{1,0:T(8,128)S(1)}, f32[1024,384]{1,0:T(8,128)S(1)}, f32[1...) custom-call(bf16[256,384]{1,0:T(8,128)(2,1)S(1)} %get-tuple-element., ...), custom_call_target="tpu_custom_call", output_to_operand_aliasing={{1}: (7, {}), {2}: (8, {}), {3}: (9, {}), {4}: (10, {})} | custom-call | flops 68719476736 | bytes 1024 | tf_op jit(solution)/shard_map/attend_back_1/pallas_call | solution.py:87
  134.1 7.7 %collective-permute-done.19.refs_1_ = f32[4,32,896]{2,1,0:T(8,128)S(1)} collective-permute-done((f32[4,32,896]{2,1,0:T(8,128)S(1)}, f32[4,32,896]{2,1,0:T(8,128)S(1)}, u32[]{:S(2)}, u32[]{:S(2)}) %collective-permute-start.19) | collective-permute-done | bytes 458784 | tf_op jit(solution)/shard_map/ppermute | solution.py:786
  143.3 4.7 %collective-permute-done.18.refs_1_ = f32[2,48,1536]{2,1,0:T(8,128)S(1)} collective-permute-done((f32[2,48,1536]{2,1,0:T(8,128)S(1)}, f32[2,48,1536]{2,1,0:T(8,128)S(1)}, u32[]{:S(2)}, u32[]{:S(2)}) %collective-permute-start.18) | collective-permute-done | bytes 589856 | tf_op jit(solution)/shard_map/ppermute | solution.py:786
  148.0 6.3 %collective-permute-done.17.refs_1_ = f32[4,48,768]{2,1,0:T(8,128)S(1)} collective-permute-done((f32[4,48,768]{2,1,0:T(8,128)S(1)}, f32[4,48,768]{2,1,0:T(8,128)S(1)}, u32[]{:S(2)}, u32[]{:S(2)}) %collective-permute-start.17) | collective-permute-done | bytes 589856 | tf_op jit(solution)/shard_map/ppermute | solution.py:786
  154.4 5.4 %collective-permute-done.22.refs_1_ = f32[2,32,896]{2,1,0:T(8,128)S(1)} collective-permute-done((f32[2,32,896]{2,1,0:T(8,128)S(1)}, f32[2,32,896]{2,1,0:T(8,128)S(1)}, u32[]{:S(2)}, u32[]{:S(2)}) %collective-permute-start.22) | collective-permute-done | bytes 229408 | tf_op jit(solution)/shard_map/ppermute | solution.py:786
  159.9 3.1 %collective-permute-start.23 = (f32[2,32,896]{2,1,0:T(8,128)S(1)}, f32[2,32,896]{2,1,0:T(8,128)S(1)}, u32[]{:S(2)}, u32[]{:S(2)}) collective-permute-start(f32[2,32,896]{2,1,0:T(8,128)S(1)} %rel_4.1.refs_2_.refs_0_), channel_id=1, source_target_pairs={{0,16},{2,18},{4,20},{6,22},{8,24},{10,26},{12,28},{14,30},{16,0},... | collective-permute-start | bytes 688136 | tf_op jit(solution)/shard_map/ppermute | solution.py:786
  163.2 7.5 %collective-permute-done.23.refs_1_ = f32[2,32,896]{2,1,0:T(8,128)S(1)} collective-permute-done((f32[2,32,896]{2,1,0:T(8,128)S(1)}, f32[2,32,896]{2,1,0:T(8,128)S(1)}, u32[]{:S(2)}, u32[]{:S(2)}) %collective-permute-start.23) | collective-permute-done | bytes 229408 | tf_op jit(solution)/shard_map/ppermute | solution.py:786
  171.7 4.9 %collective-permute-done.25.refs_1_ = f32[2,32,768]{2,1,0:T(8,128)S(1)} collective-permute-done((f32[2,32,768]{2,1,0:T(8,128)S(1)}, f32[2,32,768]{2,1,0:T(8,128)S(1)}, u32[]{:S(2)}, u32[]{:S(2)}) %collective-permute-start.25) | collective-permute-done | bytes 196640 | tf_op jit(solution)/shard_map/ppermute | solution.py:782
  181.8 6.7 %collective-permute-done.30.refs_1_ = f32[1,48,768]{2,1,0:T(8,128)S(1)} collective-permute-done((f32[1,48,768]{2,1,0:T(8,128)S(1)}, f32[1,48,768]{2,1,0:T(8,128)S(1)}, u32[]{:S(2)}, u32[]{:S(2)}) %collective-permute-start.30) | collective-permute-done | bytes 147488 | tf_op jit(solution)/shard_map/ppermute | solution.py:786
  193.5 8.0 %collective-permute-done.20.refs_1_ = f32[2,48,768]{2,1,0:T(8,128)S(1)} collective-permute-done((f32[2,48,768]{2,1,0:T(8,128)S(1)}, f32[2,48,768]{2,1,0:T(8,128)S(1)}, u32[]{:S(2)}, u32[]{:S(2)}) %collective-permute-start.20) | collective-permute-done | bytes 294944 | tf_op jit(solution)/shard_map/ppermute | solution.py:786
  205.7 8.9 %collective-permute-done.31.refs_1_ = f32[1,48,768]{2,1,0:T(8,128)S(1)} collective-permute-done((f32[1,48,768]{2,1,0:T(8,128)S(1)}, f32[1,48,768]{2,1,0:T(8,128)S(1)}, u32[]{:S(2)}, u32[]{:S(2)}) %collective-permute-start.31) | collective-permute-done | bytes 147488 | tf_op jit(solution)/shard_map/ppermute | solution.py:786
  (175 shorter events, 58.3 us)
Async XLA Ops:
  5.7 10.7 %collective-permute-start = (f32[96,768]{1,0:T(8,128)S(1)}, f32[96,768]{1,0:T(8,128)S(1)}, u32[]{:S(2)}, u32[]{:S(2)}) collective-permute-start(f32[96,768]{1,0:T(8,128)S(1)} %get-tuple-element.133.refs_6_), channel_id=1, source_target_pairs={{0,1},{1,0},{2,3},{3,2},{4,5},{5,4},{6,7},{7,6},{8,9},{9,8},{10,11... | collective-permute-start | bytes 884744 | tf_op jit(solution)/shard_map/ppermute | solution.py:782
  16.4 11.0 %collective-permute-start.2 = (f32[96,768]{1,0:T(8,128)S(1)}, f32[96,768]{1,0:T(8,128)S(1)}, u32[]{:S(2)}, u32[]{:S(2)}) collective-permute-start(f32[96,768]{1,0:T(8,128)S(1)} %collective-permute-done.refs_1_), channel_id=1, source_target_pairs={{0,4},{2,6},{4,0},{6,2},{8,12},{10,14},{12,8},{14,10},{16,20},{18,... | collective-permute-start | bytes 884744 | tf_op jit(solution)/shard_map/ppermute | solution.py:786
  18.0 11.5 %collective-permute-start.5 = (f32[256,384]{1,0:T(8,128)S(1)}, f32[256,384]{1,0:T(8,128)S(1)}, u32[]{:S(2)}, u32[]{:S(2)}) collective-permute-start(f32[256,384]{1,0:T(8,128)S(1)} %get-tuple-element.142.refs_6_.refs_8_.refs_3_), channel_id=1, source_target_pairs={{0,1},{1,0},{2,3},{3,2},{4,5},{5,4},{6,7},{7,6},{8,9},{9,8},{10,11... | collective-permute-start | bytes 1179656 | tf_op jit(solution)/shard_map/ppermute | solution.py:782
  26.3 11.9 %collective-permute-start.4 = (f32[256,384]{1,0:T(8,128)S(1)}, f32[256,384]{1,0:T(8,128)S(1)}, u32[]{:S(2)}, u32[]{:S(2)}) collective-permute-start(f32[256,384]{1,0:T(8,128)S(1)} %get-tuple-element.141.refs_5_.refs_8_), channel_id=1, source_target_pairs={{0,1},{1,0},{2,3},{3,2},{4,5},{5,4},{6,7},{7,6},{8,9},{9,8},{10,11... | collective-permute-start | bytes 1179656 | tf_op jit(solution)/shard_map/ppermute | solution.py:782
  32.4 22.7 %collective-permute-start.7 = (f32[256,768]{1,0:T(8,128)S(1)}, f32[256,768]{1,0:T(8,128)S(1)}, u32[]{:S(2)}, u32[]{:S(2)}) collective-permute-start(f32[256,768]{1,0:T(8,128)S(1)} %get-tuple-element.147.refs_0_), channel_id=1, source_target_pairs={{0,1},{1,0},{2,3},{3,2},{4,5},{5,4},{6,7},{7,6},{8,9},{9,8},{10,11... | collective-permute-start | bytes 2359304 | tf_op jit(solution)/shard_map/ppermute | solution.py:782
  41.0 30.9 %collective-permute-start.6 = (f32[256,768]{1,0:T(8,128)S(1)}, f32[256,768]{1,0:T(8,128)S(1)}, u32[]{:S(2)}, u32[]{:S(2)}) collective-permute-start(f32[256,768]{1,0:T(8,128)S(1)} %get-tuple-element.144.refs_0_), channel_id=1, source_target_pairs={{0,1},{1,0},{2,3},{3,2},{4,5},{5,4},{6,7},{7,6},{8,9},{9,8},{10,11... | collective-permute-start | bytes 2359304 | tf_op jit(solution)/shard_map/ppermute | solution.py:782
  57.4 31.3 %collective-permute-start.9 = (f32[256,768]{1,0:T(8,128)S(1)}, f32[256,768]{1,0:T(8,128)S(1)}, u32[]{:S(2)}, u32[]{:S(2)}) collective-permute-start(f32[256,768]{1,0:T(8,128)S(1)} %get-tuple-element.156.refs_0_), channel_id=1, source_target_pairs={{0,1},{1,0},{2,3},{3,2},{4,5},{5,4},{6,7},{7,6},{8,9},{9,8},{10,11... | collective-permute-start | bytes 2359304 | tf_op jit(solution)/shard_map/ppermute | solution.py:782
  77.8 11.8 %collective-permute-start.11 = (f32[8,48,1536]{2,1,0:T(8,128)S(1)}, f32[8,48,1536]{2,1,0:T(8,128)S(1)}, u32[]{:S(2)}, u32[]{:S(2)}) collective-permute-start(f32[8,48,1536]{2,1,0:T(8,128)S(1)} %get-tuple-element.172), channel_id=1, source_target_pairs={{0,2},{2,0},{4,6},{6,4},{8,10},{10,8},{12,14},{14,12},{16,18},{18,... | collective-permute-start | bytes 7077896 | tf_op jit(solution)/shard_map/ppermute | solution.py:786
  80.9 10.6 %collective-permute-start.10 = (f32[8,48,1536]{2,1,0:T(8,128)S(1)}, f32[8,48,1536]{2,1,0:T(8,128)S(1)}, u32[]{:S(2)}, u32[]{:S(2)}) collective-permute-start(f32[8,48,1536]{2,1,0:T(8,128)S(1)} %get-tuple-element.171), channel_id=1, source_target_pairs={{0,2},{2,0},{4,6},{6,4},{8,10},{10,8},{12,14},{14,12},{16,18},{18,... | collective-permute-start | bytes 7077896 | tf_op jit(solution)/shard_map/ppermute | solution.py:786
  81.4 22.7 %collective-permute-start.8 = (f32[256,768]{1,0:T(8,128)S(1)}, f32[256,768]{1,0:T(8,128)S(1)}, u32[]{:S(2)}, u32[]{:S(2)}) collective-permute-start(f32[256,768]{1,0:T(8,128)S(1)} %get-tuple-element.154.refs_0_), channel_id=1, source_target_pairs={{0,1},{1,0},{2,3},{3,2},{4,5},{5,4},{6,7},{7,6},{8,9},{9,8},{10,11... | collective-permute-start | bytes 2359304 | tf_op jit(solution)/shard_map/ppermute | solution.py:782
  90.9 32.0 %collective-permute-start.16 = (f32[4,48,1536]{2,1,0:T(8,128)}, f32[4,48,1536]{2,1,0:T(8,128)}, u32[]{:S(2)}, u32[]{:S(2)}) collective-permute-start(f32[4,48,1536]{2,1,0:T(8,128)} %get-tuple-element.202), channel_id=1, source_target_pairs={{0,4},{2,6},{4,0},{6,2},{8,12},{10,14},{12,8},{14,10},{16,20},{18,... | collective-permute-start | bytes 3538952 | tf_op jit(solution)/shard_map/ppermute | solution.py:786
  92.8 33.2 %collective-permute-start.15 = (f32[4,48,1536]{2,1,0:T(8,128)}, f32[4,48,1536]{2,1,0:T(8,128)}, u32[]{:S(2)}, u32[]{:S(2)}) collective-permute-start(f32[4,48,1536]{2,1,0:T(8,128)} %get-tuple-element.201), channel_id=1, source_target_pairs={{0,8},{2,10},{4,12},{6,14},{8,0},{10,2},{12,4},{14,6},{16,24},{18,... | collective-permute-start | bytes 3538952 | tf_op jit(solution)/shard_map/ppermute | solution.py:786
  124.3 23.7 %collective-permute-start.18 = (f32[2,48,1536]{2,1,0:T(8,128)S(1)}, f32[2,48,1536]{2,1,0:T(8,128)S(1)}, u32[]{:S(2)}, u32[]{:S(2)}) collective-permute-start(f32[2,48,1536]{2,1,0:T(8,128)S(1)} %get-tuple-element.208), channel_id=1, source_target_pairs={{0,8},{2,10},{4,12},{6,14},{8,0},{10,2},{12,4},{14,6},{16,24},{18,... | collective-permute-start | bytes 1769480 | tf_op jit(solution)/shard_map/ppermute | solution.py:786
  128.3 13.4 %collective-permute-start.19 = (f32[4,32,896]{2,1,0:T(8,128)S(1)}, f32[4,32,896]{2,1,0:T(8,128)S(1)}, u32[]{:S(2)}, u32[]{:S(2)}) collective-permute-start(f32[4,32,896]{2,1,0:T(8,128)S(1)} %get-tuple-element.209), channel_id=1, source_target_pairs={{0,4},{2,6},{4,0},{6,2},{8,12},{10,14},{12,8},{14,10},{16,20},{18,... | collective-permute-start | bytes 1376264 | tf_op jit(solution)/shard_map/ppermute | solution.py:786
  130.2 24.2 %collective-permute-start.17 = (f32[4,48,768]{2,1,0:T(8,128)S(1)}, f32[4,48,768]{2,1,0:T(8,128)S(1)}, u32[]{:S(2)}, u32[]{:S(2)}) collective-permute-start(f32[4,48,768]{2,1,0:T(8,128)S(1)} %get-tuple-element.207), channel_id=1, source_target_pairs={{0,4},{2,6},{4,0},{6,2},{8,12},{10,14},{12,8},{14,10},{16,20},{18,... | collective-permute-start | bytes 1769480 | tf_op jit(solution)/shard_map/ppermute | solution.py:786
  130.8 62.7 %collective-permute-start.21 = (f32[512,768]{1,0:T(8,128)S(1)}, f32[512,768]{1,0:T(8,128)S(1)}, u32[]{:S(2)}, u32[]{:S(2)}) collective-permute-start(f32[512,768]{1,0:T(8,128)S(1)} %hidden_grad.1.refs_15_.refs_2_), channel_id=1, source_target_pairs={{0,1},{1,0},{2,3},{3,2},{4,5},{5,4},{6,7},{7,6},{8,9},{9,8},{10,11... | collective-permute-start | bytes 4718600 | tf_op jit(solution)/shard_map/ppermute | solution.py:782
  131.5 31.6 %collective-permute-start.24 = (f32[2,48,1536]{2,1,0:T(8,128)S(1)}, f32[2,48,1536]{2,1,0:T(8,128)S(1)}, u32[]{:S(2)}, u32[]{:S(2)}) collective-permute-start(f32[2,48,1536]{2,1,0:T(8,128)S(1)} %get-tuple-element.217), channel_id=1, source_target_pairs={{0,16},{2,18},{4,20},{6,22},{8,24},{10,26},{12,28},{14,30},{16,0},... | collective-permute-start | bytes 1769480 | tf_op jit(solution)/shard_map/ppermute | solution.py:786
  141.7 29.0 %collective-permute-start.26 = (f32[4,48,768]{2,1,0:T(8,128)S(1)}, f32[4,48,768]{2,1,0:T(8,128)S(1)}, u32[]{:S(2)}, u32[]{:S(2)}) collective-permute-start(f32[4,48,768]{2,1,0:T(8,128)S(1)} %get-tuple-element.222), channel_id=1, source_target_pairs={{0,4},{2,6},{4,0},{6,2},{8,12},{10,14},{12,8},{14,10},{16,20},{18,... | collective-permute-start | bytes 1769480 | tf_op jit(solution)/shard_map/ppermute | solution.py:786
  148.0 11.9 %collective-permute-start.22 = (f32[2,32,896]{2,1,0:T(8,128)S(1)}, f32[2,32,896]{2,1,0:T(8,128)S(1)}, u32[]{:S(2)}, u32[]{:S(2)}) collective-permute-start(f32[2,32,896]{2,1,0:T(8,128)S(1)} %get-tuple-element.216), channel_id=1, source_target_pairs={{0,8},{2,10},{4,12},{6,14},{8,0},{10,2},{12,4},{14,6},{16,24},{18,... | collective-permute-start | bytes 688136 | tf_op jit(solution)/shard_map/ppermute | solution.py:786
  159.9 10.8 %collective-permute-start.23 = (f32[2,32,896]{2,1,0:T(8,128)S(1)}, f32[2,32,896]{2,1,0:T(8,128)S(1)}, u32[]{:S(2)}, u32[]{:S(2)}) collective-permute-start(f32[2,32,896]{2,1,0:T(8,128)S(1)} %rel_4.1.refs_2_.refs_0_), channel_id=1, source_target_pairs={{0,16},{2,18},{4,20},{6,22},{8,24},{10,26},{12,28},{14,30},{16,0},... | collective-permute-start | bytes 688136 | tf_op jit(solution)/shard_map/ppermute | solution.py:786
  163.1 15.6 %collective-permute-start.29 = (f32[1,48,1536]{2,1,0:T(8,128)S(1)}, f32[1,48,1536]{2,1,0:T(8,128)S(1)}, u32[]{:S(2)}, u32[]{:S(2)}) collective-permute-start(f32[1,48,1536]{2,1,0:T(8,128)S(1)} %get-tuple-element.225), channel_id=1, source_target_pairs={{0,4},{2,6},{4,0},{6,2},{8,12},{10,14},{12,8},{14,10},{16,20},{18,... | collective-permute-start | bytes 884744 | tf_op jit(solution)/shard_map/ppermute | solution.py:786
  176.7 12.5 %collective-permute-start.27 = (f32[2,32,896]{2,1,0:T(8,128)S(1)}, f32[2,32,896]{2,1,0:T(8,128)S(1)}, u32[]{:S(2)}, u32[]{:S(2)}) collective-permute-start(f32[2,32,896]{2,1,0:T(8,128)S(1)} %rel_join.1.refs_2_.refs_0_), channel_id=1, source_target_pairs={{0,8},{2,10},{4,12},{6,14},{8,0},{10,2},{12,4},{14,6},{16,24},{18,... | collective-permute-start | bytes 688136 | tf_op jit(solution)/shard_map/ppermute | solution.py:786
  190.1 14.1 %collective-permute-start.32 = (f32[4,32,896]{2,1,0:T(8,128)S(1)}, f32[4,32,896]{2,1,0:T(8,128)S(1)}, u32[]{:S(2)}, u32[]{:S(2)}) collective-permute-start(f32[4,32,896]{2,1,0:T(8,128)S(1)} %pack_4.1.refs_6_), channel_id=1, source_target_pairs={{0,4},{2,6},{4,0},{6,2},{8,12},{10,14},{12,8},{14,10},{16,20},{18,... | collective-permute-start | bytes 1376264 | tf_op jit(solution)/shard_map/ppermute | solution.py:786
  191.7 11.8 %collective-permute-start.33 = (f32[1,48,1536]{2,1,0:T(8,128)S(1)}, f32[1,48,1536]{2,1,0:T(8,128)S(1)}, u32[]{:S(2)}, u32[]{:S(2)}) collective-permute-start(f32[1,48,1536]{2,1,0:T(8,128)S(1)} %get-tuple-element.232), channel_id=1, source_target_pairs={{0,16},{2,18},{4,20},{6,22},{8,24},{10,26},{12,28},{14,30},{16,0},... | collective-permute-start | bytes 884744 | tf_op jit(solution)/shard_map/ppermute | solution.py:786
  (55 other events, 423.8 us)
where the time goes:
time: 217 us; the launch traced here: 216 us
  waiting for transfers between devices  103 us (47%)
  Pallas kernels  75.6 us (35%)
  starting transfers between devices  32.2 us (15%)
  local copies, waits for them, and re-layouts  3.07 us (1%)
  between operations  2.27 us (1%)
    pallas_call x40, Pallas kernels, call(): pl.pallas_call(body, in_specs=in_specs, out_specs=[pl.BlockSpec() if at i...  75.6 us
    ppermute x26, waiting for transfers between devices, flip(): return lax.ppermute(value, 'dp', [(i, i ^ bit) for i in range(parts)])  58.8 us
    ppermute x9, waiting for transfers between devices, swap_head(): return lax.ppermute(value, 'head', [(0, 1), (1, 0)])  44.3 us
    ppermute x26, starting transfers between devices, flip(): return lax.ppermute(value, 'dp', [(i, i ^ bit) for i in range(parts)])  23.3 us
    ppermute x9, starting transfers between devices, swap_head(): return lax.ppermute(value, 'head', [(0, 1), (1, 0)])  8.91 us
  transfers between devices with their start and end apart: 35, of which 18 were waited for; matrix products, arithmetic and copies ran while one was open for 0% of the time, Pallas kernels for 32%

commit v1 on v0

--- a/solution.py
+++ b/solution.py
@@ -18,8 +18,8 @@
 LANES = 128
 STREAMS = 2
 CONTEXTS = 1
-TAIL = "YLKGDIR(VQ)RDVXISQJiQqP(VH)dP(vU)"
-REL_PIECES = 1
+TAIL = "LYKGDIR(VQ)RDVXISQJiQqP(VH)dP(vU)"
+REL_PIECES = 2
 HEAD_PIECES = 1
 QUARTERS = 4
 COLUMNS = 384
@@ -435,7 +435,7 @@
     wdown_ref, *refs,
 ):
     own_refs, other_refs = refs[:count], refs[count : 2 * count]
-    xhat_ref, rstd_ref, normed_ref, act_ref, slope_ref, low_ref = refs[2 * count :]
+    xhat_ref, rstd_ref, normed_ref, act_ref, slope_ref, low_ref, bias_ref = refs[2 * count :]
     own = jnp.concatenate([ref[...] for ref in own_refs], axis=0)
     other = jnp.concatenate([ref[...] for ref in other_refs], axis=0)
     first = lax.axis_index("head") == 0
@@ -455,19 +455,19 @@
     normed_ref[...] = low
     units = win_ref.shape[1]
     step = units // 3
-    total = None
-    bias = bin_ref[...].astype(F32)[None, :]
-    for part in range(3):
-        cols = slice(part * step, (part + 1) * step)
-        inner = dot_nn(low, win_ref[:, cols]) + bias[:, cols]
+    bias_ref[...] = bin_ref[...].astype(F32)[None, :]
+    low_ref[...] = jnp.zeros_like(low_ref)
+
+    @pl.loop(0, 3)
+    def _(part):
+        cols = pl.ds(pl.multiple_of(part * step, step), step)
+        inner = dot_nn(low, win_ref[:, cols]) + bias_ref[:, cols]
         phi = 0.5 * (1.0 + lax.erf(inner * math.sqrt(0.5)))
         act = (inner * phi).astype(BF16)
         slope = phi + inner * (jnp.exp(-0.5 * inner * inner) * (1.0 / math.sqrt(2 * math.pi)))
         act_ref[:, cols] = act
         slope_ref[:, cols] = slope
-        term = dot_nn(act, wdown_ref[cols, :])
-        total = term if total is None else total + term
-    low_ref[...] = total
+        low_ref[...] += dot_nn(act, wdown_ref[cols, :])
 
 
 def feed(line, at, height, own, other, wout, bout, hidden, gain, shift, win, b_in, wdown):
@@ -484,7 +484,7 @@
     operands = (wout, bout, hidden, gain, shift, win, b_in, wdown, *own, *other)
     return line.call(
         functools.partial(feed_kernel, at, height, len(own)), f"feed_{at}", outs, operands,
-        flops=BACK_FLOPS if at else 1024,
+        scratch=[pltpu.VMEM((1, units), F32)], flops=BACK_FLOPS if at else 1024,
     )
 
 
@@ -494,7 +494,7 @@
     *refs,
 ):
     before, refs = refs[:count], refs[count:]
-    out_ref, d_two_ref, d_low_ref, d_inner_ref, vec_ref, bin_ref, *dn_refs = refs
+    out_ref, d_two_ref, d_low_ref, d_inner_ref, vec_ref, bin_ref, dn_ref = refs
     normed = xhat_one_ref[...] * gain_one_ref[...].astype(F32)[None, :]
     normed = normed + shift_one_ref[...].astype(F32)[None, :]
     resid = (low_own_ref[...] + low_other_ref[...]) + bdown_ref[...].astype(F32)[None, :] + normed
@@ -523,18 +523,16 @@
     d_low_ref[...] = low
     units = win_ref.shape[1]
     step = units // 3
-    total = None
-    for part in range(3):
-        cols = slice(part * step, (part + 1) * step)
+    dn_ref[...] = jnp.zeros_like(dn_ref)
+
+    @pl.loop(0, 3)
+    def _(part):
+        cols = pl.ds(pl.multiple_of(part * step, step), step)
         d_act = dot_nt(low, wdown_ref[cols, :])
         d_inner = (d_act * slope_ref[:, cols]).astype(BF16)
         d_inner_ref[:, cols] = d_inner
         bin_ref[0:1, cols] = jnp.sum(d_inner.astype(F32), axis=0, keepdims=True)
-        term = dot_nt(d_inner, win_ref[:, cols])
-        total = term if total is None else total + term
-    rows = dn_refs[0].shape[0]
-    for piece, ref in enumerate(dn_refs):
-        ref[...] = total[piece * rows : (piece + 1) * rows]
+        dn_ref[...] += dot_nt(d_inner, win_ref[:, cols])
 
 
 def feed_back(

time: 217 us -> 216 us (level)
    ppermute x26 -> x27, starting transfers between devices: 23.3 us -> 22.2 us  [flip(): return lax.ppermute(value, 'dp', [(i, i ^ bit) for i in range(parts)])]
    ppermute x26 -> x27, waiting for transfers between devices: 58.8 us -> 59.8 us  [flip(): return lax.ppermute(value, 'dp', [(i, i ^ bit) for i in range(parts)])]
  transfers between devices with their start and end apart: 35 -> 36, of which waited for: 18 -> 19; matrix products, arithmetic and copies ran while one was open for 0% -> 0% of each run, Pallas kernels for 32% -> 33%
where the time goes in v1:
time: 216 us
  waiting for transfers between devices  103 us (48%)
  Pallas kernels  77.3 us (36%)
  starting transfers between devices  30.6 us (14%)
  local copies, waits for them, and re-layouts  3.07 us (1%)
  between operations  2.3 us (1%)
    pallas_call x40, Pallas kernels, call(): pl.pallas_call(body, in_specs=in_specs, out_specs=[pl.BlockSpec() if at i...  77.3 us
    ppermute x27, waiting for transfers between devices, flip(): return lax.ppermute(value, 'dp', [(i, i ^ bit) for i in range(parts)])  59.8 us
    ppermute x9, waiting for transfers between devices, swap_head(): return lax.ppermute(value, 'head', [(0, 1), (1, 0)])  42.9 us
    ppermute x27, starting transfers between devices, flip(): return lax.ppermute(value, 'dp', [(i, i ^ bit) for i in range(parts)])  22.2 us
    ppermute x9, starting transfers between devices, swap_head(): return lax.ppermute(value, 'head', [(0, 1), (1, 0)])  8.39 us
  transfers between devices with their start and end apart: 36, of which 19 were waited for; matrix products, arithmetic and copies ran while one was open for 0% of the time, Pallas kernels for 33%

profile of v1, /device:TPU:0, one launch (start us, length us, event | category | flops | bytes accessed | tf_op | source)
XLA Modules:
  0.0 215.9 jit_solution(7058691364914227643)
XLA Ops:
  0.7 5.0 %project.1 = (bf16[512,384]{1,0:T(8,128)(2,1)S(1)}, bf16[512,384]{1,0:T(8,128)(2,1)S(1)}, bf16[512,384]{1,0:T(8,128)(2,1)S(1)}, bf16[1024,384]{1,0:T(8,128)(2,1)...) custom-call(s32[1,1024]{1,0:T(1,128)} %constant.2.clone.refs_0_, bf16[512,768]{1,0:T(8,128)(2,1)} %refs_0_.7, ...), custom_call_target="tpu_custom_call" | custom-call | flops 1024 | bytes 1024 | tf_op jit(solution)/shard_map/project/pallas_call | solution.py:87
  5.7 3.0 %collective-permute-start = (f32[96,768]{1,0:T(8,128)S(1)}, f32[96,768]{1,0:T(8,128)S(1)}, u32[]{:S(2)}, u32[]{:S(2)}) collective-permute-start(f32[96,768]{1,0:T(8,128)S(1)} %get-tuple-element.134.refs_6_), channel_id=1, source_target_pairs={{0,1},{1,0},{2,3},{3,2},{4,5},{5,4},{6,7},{7,6},{8,9},{9,8},{10,11... | collective-permute-start | bytes 884744 | tf_op jit(solution)/shard_map/ppermute | solution.py:780
  9.4 7.2 %attend_0.1 = (f32[256,384]{1,0:T(8,128)S(1)}, bf16[6,256,512]{2,1,0:T(8,128)(2,1)S(1)}) custom-call(s32[1]{0:T(128)S(6)} %copy.48.refs_0_, bf16[512,384]{1,0:T(8,128)(2,1)S(1)} %get-tuple-element.135.refs_1_, bf16[512,384]{1,0:T(8,128)(2,1)S(1)} %get-tuple-element.136.refs_2_, bf16[512,384]{1,0:T(8,128)(2,1)S(1)} %get-tuple-element.137.refs_3_, ...), custom_call_target="tpu_custom_call" | custom-call | flops 1024 | bytes 1024 | tf_op jit(solution)/shard_map/attend_0/pallas_call | solution.py:87
  19.0 7.0 %attend_1.1 = (f32[256,384]{1,0:T(8,128)S(1)}, bf16[6,256,512]{2,1,0:T(8,128)(2,1)S(1)}) custom-call(s32[1]{0:T(128)S(6)} %copy.48.refs_0_, bf16[512,384]{1,0:T(8,128)(2,1)S(1)} %get-tuple-element.135.refs_1_, bf16[512,384]{1,0:T(8,128)(2,1)S(1)} %get-tuple-element.136.refs_2_, bf16[512,384]{1,0:T(8,128)(2,1)S(1)} %get-tuple-element.137.refs_3_, ...), custom_call_target="tpu_custom_call" | custom-call | flops 1024 | bytes 1024 | tf_op jit(solution)/shard_map/attend_1/pallas_call | solution.py:87
  29.6 3.1 %feed_0.1 = (f32[256,768]{1,0:T(8,128)S(1)}, f32[256,1]{1,0:T(8,128)S(1)}, bf16[256,768]{1,0:T(8,128)(2,1)S(1)}, bf16[256,1536]{1,0:T(8,128)(2,1)S(1)}, f32[256,1536]{1,0:T(8,128)S(1)}, /*index=5*/f32[256,768]{1,0:T(8,128)S(1)}) custom-call(bf16[768,768]{1,0:T(8,128)(2,1)S(1)} %bitcast.4, bf16[768]{0:T(1024)(128)(2,1)S(1)} %copy-done.43, ...), custom_call_target="tpu_custom_call" | custom-call | flops 1024 | bytes 1024 | tf_op jit(solution)/shard_map/feed_0/pallas_call | solution.py:87
  33.6 4.6 %collective-permute-done.4.refs_9_ = f32[256,384]{1,0:T(8,128)S(1)} collective-permute-done((f32[256,384]{1,0:T(8,128)S(1)}, f32[256,384]{1,0:T(8,128)S(1)}, u32[]{:S(2)}, u32[]{:S(2)}) %collective-permute-start.4) | collective-permute-done | bytes 393248 | tf_op jit(solution)/shard_map/ppermute | solution.py:780
  38.3 3.1 %feed_1.1 = (f32[256,768]{1,0:T(8,128)S(1)}, f32[256,1]{1,0:T(8,128)S(1)}, bf16[256,768]{1,0:T(8,128)(2,1)S(1)}, bf16[256,1536]{1,0:T(8,128)(2,1)S(1)}, f32[256,1536]{1,0:T(8,128)S(1)}, /*index=5*/f32[256,768]{1,0:T(8,128)S(1)}) custom-call(bf16[768,768]{1,0:T(8,128)(2,1)S(1)} %bitcast.5, bf16[768]{0:T(1024)(128)(2,1)S(1)} %copy-done.43, ...), custom_call_target="tpu_custom_call" | custom-call | flops 68719476736 | bytes 1024 | tf_op jit(solution)/shard_map/feed_1/pallas_call | solution.py:87
  41.7 13.4 %collective-permute-done.7.refs_1_ = f32[256,768]{1,0:T(8,128)S(1)} collective-permute-done((f32[256,768]{1,0:T(8,128)S(1)}, f32[256,768]{1,0:T(8,128)S(1)}, u32[]{:S(2)}, u32[]{:S(2)}) %collective-permute-start.7) | collective-permute-done | bytes 786464 | tf_op jit(solution)/shard_map/ppermute | solution.py:780
  55.1 3.1 %feed_back_0.1 = (bf16[256,768]{1,0:T(8,128)(2,1)S(1)}, f32[256,768]{1,0:T(8,128)S(1)}, bf16[256,768]{1,0:T(8,128)(2,1)S(1)}, bf16[256,1536]{1,0:T(8,128)(2,1)S(...) custom-call(f32[256,768]{1,0:T(8,128)S(1)} %get-tuple-element.148.refs_0_, ...), custom_call_target="tpu_custom_call" | custom-call | flops 1024 | bytes 1024 | tf_op jit(solution)/shard_map/feed_back_0/pallas_call | solution.py:87
  58.6 13.4 %collective-permute-done.6.refs_1_ = f32[256,768]{1,0:T(8,128)S(1)} collective-permute-done((f32[256,768]{1,0:T(8,128)S(1)}, f32[256,768]{1,0:T(8,128)S(1)}, u32[]{:S(2)}, u32[]{:S(2)}) %collective-permute-start.6) | collective-permute-done | bytes 786464 | tf_op jit(solution)/shard_map/ppermute | solution.py:780
  72.0 3.8 %feed_back_1.1 = (bf16[512,768]{1,0:T(8,128)(2,1)}, f32[256,768]{1,0:T(8,128)S(1)}, bf16[256,768]{1,0:T(8,128)(2,1)S(1)}, bf16[256,1536]{1,0:T(8,128)(2,1)S(1)},...) custom-call(f32[256,768]{1,0:T(8,128)S(1)} %get-tuple-element.145.refs_0_, ...), custom_call_target="tpu_custom_call" | custom-call | flops 1024 | bytes 1024 | tf_op jit(solution)/shard_map/feed_back_1/pallas_call | solution.py:87
  78.6 3.0 %grad_in.1 = (f32[8,48,1536]{2,1,0:T(8,128)S(1)}, f32[8,48,1536]{2,1,0:T(8,128)S(1)}) custom-call(bf16[256,768]{1,0:T(8,128)(2,1)S(1)} %get-tuple-element.159.refs_0_, bf16[256,1536]{1,0:T(8,128)(2,1)S(1)} %get-tuple-element.160.refs_1_, bf16[256,768]{1,0:T(8,128)(2,1)S(1)} %get-tuple-element.161.refs_2_, bf16[256,1536]{1,0:T(8,128)(2,1)S(1)} %get-tuple-element.162.refs_3_, ...), custom_call_target="tpu_custom_call" | custom-call | flops 1024 | bytes 1024 | tf_op jit(solution)/shard_map/grad_in/pallas_call | solution.py:87
  82.3 6.5 %collective-permute-done.9.refs_1_ = f32[256,768]{1,0:T(8,128)S(1)} collective-permute-done((f32[256,768]{1,0:T(8,128)S(1)}, f32[256,768]{1,0:T(8,128)S(1)}, u32[]{:S(2)}, u32[]{:S(2)}) %collective-permute-start.9) | collective-permute-done | bytes 786464 | tf_op jit(solution)/shard_map/ppermute | solution.py:780
  94.4 9.7 %attend_back_0.1 = (bf16[256,384]{1,0:T(8,128)(2,1)S(1)}, f32[512,384]{1,0:T(8,128)S(1)}, f32[512,384]{1,0:T(8,128)S(1)}, f32[1024,384]{1,0:T(8,128)S(1)}, f32[1024,384]{1,0:T(8,128)S(1)}) custom-call(bf16[256,384]{1,0:T(8,128)(2,1)S(1)} %get-tuple-element.170.refs_0_, bf16[512,384]{1,0:T(8,128)(2,1)S(1)} %copy-done.18, bf16[512,384]{1,0:T(8,128)(2,1)S(1)} %copy-done.20, ...), custom_call_target="tpu_custom_call" | custom-call | flops 68719476736 | bytes 1024 | tf_op jit(solution)/shard_map/attend_back_0/pallas_call | solution.py:87
  105.2 9.5 %attend_back_1.1 = (bf16[256,384]{1,0:T(8,128)(2,1)S(1)}, f32[512,384]{1,0:T(8,128)S(1)}, f32[512,384]{1,0:T(8,128)S(1)}, f32[1024,384]{1,0:T(8,128)S(1)}, f32[1...) custom-call(bf16[256,384]{1,0:T(8,128)(2,1)S(1)} %get-tuple-element., ...), custom_call_target="tpu_custom_call", output_to_operand_aliasing={{1}: (7, {}), {2}: (8, {}), {3}: (9, {}), {4}: (10, {})} | custom-call | flops 68719476736 | bytes 1024 | tf_op jit(solution)/shard_map/attend_back_1/pallas_call | solution.py:87
  134.0 7.9 %collective-permute-done.20.refs_1_ = f32[4,32,896]{2,1,0:T(8,128)S(1)} collective-permute-done((f32[4,32,896]{2,1,0:T(8,128)S(1)}, f32[4,32,896]{2,1,0:T(8,128)S(1)}, u32[]{:S(2)}, u32[]{:S(2)}) %collective-permute-start.20) | collective-permute-done | bytes 458784 | tf_op jit(solution)/shard_map/ppermute | solution.py:784
  143.2 5.3 %collective-permute-done.19.refs_1_ = f32[2,48,1536]{2,1,0:T(8,128)S(1)} collective-permute-done((f32[2,48,1536]{2,1,0:T(8,128)S(1)}, f32[2,48,1536]{2,1,0:T(8,128)S(1)}, u32[]{:S(2)}, u32[]{:S(2)}) %collective-permute-start.19) | collective-permute-done | bytes 589856 | tf_op jit(solution)/shard_map/ppermute | solution.py:784
  148.5 6.0 %collective-permute-done.18.refs_1_ = f32[4,48,768]{2,1,0:T(8,128)S(1)} collective-permute-done((f32[4,48,768]{2,1,0:T(8,128)S(1)}, f32[4,48,768]{2,1,0:T(8,128)S(1)}, u32[]{:S(2)}, u32[]{:S(2)}) %collective-permute-start.18) | collective-permute-done | bytes 589856 | tf_op jit(solution)/shard_map/ppermute | solution.py:784
  154.5 5.1 %collective-permute-done.23.refs_1_ = f32[2,32,896]{2,1,0:T(8,128)S(1)} collective-permute-done((f32[2,32,896]{2,1,0:T(8,128)S(1)}, f32[2,32,896]{2,1,0:T(8,128)S(1)}, u32[]{:S(2)}, u32[]{:S(2)}) %collective-permute-start.23) | collective-permute-done | bytes 229408 | tf_op jit(solution)/shard_map/ppermute | solution.py:784
  162.0 8.5 %collective-permute-done.24.refs_1_ = f32[2,32,896]{2,1,0:T(8,128)S(1)} collective-permute-done((f32[2,32,896]{2,1,0:T(8,128)S(1)}, f32[2,32,896]{2,1,0:T(8,128)S(1)}, u32[]{:S(2)}, u32[]{:S(2)}) %collective-permute-start.24) | collective-permute-done | bytes 229408 | tf_op jit(solution)/shard_map/ppermute | solution.py:784
  171.8 4.7 %collective-permute-done.26.refs_1_ = f32[2,32,768]{2,1,0:T(8,128)S(1)} collective-permute-done((f32[2,32,768]{2,1,0:T(8,128)S(1)}, f32[2,32,768]{2,1,0:T(8,128)S(1)}, u32[]{:S(2)}, u32[]{:S(2)}) %collective-permute-start.26) | collective-permute-done | bytes 196640 | tf_op jit(solution)/shard_map/ppermute | solution.py:780
  181.4 7.0 %collective-permute-done.31.refs_1_ = f32[1,48,768]{2,1,0:T(8,128)S(1)} collective-permute-done((f32[1,48,768]{2,1,0:T(8,128)S(1)}, f32[1,48,768]{2,1,0:T(8,128)S(1)}, u32[]{:S(2)}, u32[]{:S(2)}) %collective-permute-start.31) | collective-permute-done | bytes 147488 | tf_op jit(solution)/shard_map/ppermute | solution.py:784
  193.1 7.9 %collective-permute-done.21.refs_1_ = f32[2,48,768]{2,1,0:T(8,128)S(1)} collective-permute-done((f32[2,48,768]{2,1,0:T(8,128)S(1)}, f32[2,48,768]{2,1,0:T(8,128)S(1)}, u32[]{:S(2)}, u32[]{:S(2)}) %collective-permute-start.21) | collective-permute-done | bytes 294944 | tf_op jit(solution)/shard_map/ppermute | solution.py:784
  205.3 9.0 %collective-permute-done.32.refs_1_ = f32[1,48,768]{2,1,0:T(8,128)S(1)} collective-permute-done((f32[1,48,768]{2,1,0:T(8,128)S(1)}, f32[1,48,768]{2,1,0:T(8,128)S(1)}, u32[]{:S(2)}, u32[]{:S(2)}) %collective-permute-start.32) | collective-permute-done | bytes 147488 | tf_op jit(solution)/shard_map/ppermute | solution.py:784
  (177 shorter events, 56.9 us)
Async XLA Ops:
  5.7 10.9 %collective-permute-start = (f32[96,768]{1,0:T(8,128)S(1)}, f32[96,768]{1,0:T(8,128)S(1)}, u32[]{:S(2)}, u32[]{:S(2)}) collective-permute-start(f32[96,768]{1,0:T(8,128)S(1)} %get-tuple-element.134.refs_6_), channel_id=1, source_target_pairs={{0,1},{1,0},{2,3},{3,2},{4,5},{5,4},{6,7},{7,6},{8,9},{9,8},{10,11... | collective-permute-start | bytes 884744 | tf_op jit(solution)/shard_map/ppermute | solution.py:780
  16.6 10.8 %collective-permute-start.2 = (f32[96,768]{1,0:T(8,128)S(1)}, f32[96,768]{1,0:T(8,128)S(1)}, u32[]{:S(2)}, u32[]{:S(2)}) collective-permute-start(f32[96,768]{1,0:T(8,128)S(1)} %collective-permute-done.refs_1_), channel_id=1, source_target_pairs={{0,4},{2,6},{4,0},{6,2},{8,12},{10,14},{12,8},{14,10},{16,20},{18,... | collective-permute-start | bytes 884744 | tf_op jit(solution)/shard_map/ppermute | solution.py:784
  18.2 11.3 %collective-permute-start.5 = (f32[256,384]{1,0:T(8,128)S(1)}, f32[256,384]{1,0:T(8,128)S(1)}, u32[]{:S(2)}, u32[]{:S(2)}) collective-permute-start(f32[256,384]{1,0:T(8,128)S(1)} %get-tuple-element.143.refs_6_.refs_8_.refs_3_), channel_id=1, source_target_pairs={{0,1},{1,0},{2,3},{3,2},{4,5},{5,4},{6,7},{7,6},{8,9},{9,8},{10,11... | collective-permute-start | bytes 1179656 | tf_op jit(solution)/shard_map/ppermute | solution.py:780
  26.1 12.1 %collective-permute-start.4 = (f32[256,384]{1,0:T(8,128)S(1)}, f32[256,384]{1,0:T(8,128)S(1)}, u32[]{:S(2)}, u32[]{:S(2)}) collective-permute-start(f32[256,384]{1,0:T(8,128)S(1)} %get-tuple-element.142.refs_5_.refs_8_), channel_id=1, source_target_pairs={{0,1},{1,0},{2,3},{3,2},{4,5},{5,4},{6,7},{7,6},{8,9},{9,8},{10,11... | collective-permute-start | bytes 1179656 | tf_op jit(solution)/shard_map/ppermute | solution.py:780
  32.7 22.4 %collective-permute-start.7 = (f32[256,768]{1,0:T(8,128)S(1)}, f32[256,768]{1,0:T(8,128)S(1)}, u32[]{:S(2)}, u32[]{:S(2)}) collective-permute-start(f32[256,768]{1,0:T(8,128)S(1)} %get-tuple-element.148.refs_0_), channel_id=1, source_target_pairs={{0,1},{1,0},{2,3},{3,2},{4,5},{5,4},{6,7},{7,6},{8,9},{9,8},{10,11... | collective-permute-start | bytes 2359304 | tf_op jit(solution)/shard_map/ppermute | solution.py:780
  41.4 30.5 %collective-permute-start.6 = (f32[256,768]{1,0:T(8,128)S(1)}, f32[256,768]{1,0:T(8,128)S(1)}, u32[]{:S(2)}, u32[]{:S(2)}) collective-permute-start(f32[256,768]{1,0:T(8,128)S(1)} %get-tuple-element.145.refs_0_), channel_id=1, source_target_pairs={{0,1},{1,0},{2,3},{3,2},{4,5},{5,4},{6,7},{7,6},{8,9},{9,8},{10,11... | collective-permute-start | bytes 2359304 | tf_op jit(solution)/shard_map/ppermute | solution.py:780
  58.3 30.5 %collective-permute-start.9 = (f32[256,768]{1,0:T(8,128)S(1)}, f32[256,768]{1,0:T(8,128)S(1)}, u32[]{:S(2)}, u32[]{:S(2)}) collective-permute-start(f32[256,768]{1,0:T(8,128)S(1)} %get-tuple-element.157.refs_0_), channel_id=1, source_target_pairs={{0,1},{1,0},{2,3},{3,2},{4,5},{5,4},{6,7},{7,6},{8,9},{9,8},{10,11... | collective-permute-start | bytes 2359304 | tf_op jit(solution)/shard_map/ppermute | solution.py:780
  78.5 11.2 %collective-permute-start.11 = (f32[8,48,1536]{2,1,0:T(8,128)S(1)}, f32[8,48,1536]{2,1,0:T(8,128)S(1)}, u32[]{:S(2)}, u32[]{:S(2)}) collective-permute-start(f32[8,48,1536]{2,1,0:T(8,128)S(1)} %get-tuple-element.173), channel_id=1, source_target_pairs={{0,2},{2,0},{4,6},{6,4},{8,10},{10,8},{12,14},{14,12},{16,18},{18,... | collective-permute-start | bytes 7077896 | tf_op jit(solution)/shard_map/ppermute | solution.py:784
  81.5 9.9 %collective-permute-start.10 = (f32[8,48,1536]{2,1,0:T(8,128)S(1)}, f32[8,48,1536]{2,1,0:T(8,128)S(1)}, u32[]{:S(2)}, u32[]{:S(2)}) collective-permute-start(f32[8,48,1536]{2,1,0:T(8,128)S(1)} %get-tuple-element.172), channel_id=1, source_target_pairs={{0,2},{2,0},{4,6},{6,4},{8,10},{10,8},{12,14},{14,12},{16,18},{18,... | collective-permute-start | bytes 7077896 | tf_op jit(solution)/shard_map/ppermute | solution.py:784
  82.1 22.2 %collective-permute-start.8 = (f32[256,768]{1,0:T(8,128)S(1)}, f32[256,768]{1,0:T(8,128)S(1)}, u32[]{:S(2)}, u32[]{:S(2)}) collective-permute-start(f32[256,768]{1,0:T(8,128)S(1)} %get-tuple-element.155.refs_0_), channel_id=1, source_target_pairs={{0,1},{1,0},{2,3},{3,2},{4,5},{5,4},{6,7},{7,6},{8,9},{9,8},{10,11... | collective-permute-start | bytes 2359304 | tf_op jit(solution)/shard_map/ppermute | solution.py:780
  90.9 32.1 %collective-permute-start.17 = (f32[4,48,1536]{2,1,0:T(8,128)}, f32[4,48,1536]{2,1,0:T(8,128)}, u32[]{:S(2)}, u32[]{:S(2)}) collective-permute-start(f32[4,48,1536]{2,1,0:T(8,128)} %get-tuple-element.204), channel_id=1, source_target_pairs={{0,4},{2,6},{4,0},{6,2},{8,12},{10,14},{12,8},{14,10},{16,20},{18,... | collective-permute-start | bytes 3538952 | tf_op jit(solution)/shard_map/ppermute | solution.py:784
  92.8 32.1 %collective-permute-start.16 = (f32[4,48,1536]{2,1,0:T(8,128)}, f32[4,48,1536]{2,1,0:T(8,128)}, u32[]{:S(2)}, u32[]{:S(2)}) collective-permute-start(f32[4,48,1536]{2,1,0:T(8,128)} %get-tuple-element.203), channel_id=1, source_target_pairs={{0,8},{2,10},{4,12},{6,14},{8,0},{10,2},{12,4},{14,6},{16,24},{18,... | collective-permute-start | bytes 3538952 | tf_op jit(solution)/shard_map/ppermute | solution.py:784
  124.9 23.6 %collective-permute-start.19 = (f32[2,48,1536]{2,1,0:T(8,128)S(1)}, f32[2,48,1536]{2,1,0:T(8,128)S(1)}, u32[]{:S(2)}, u32[]{:S(2)}) collective-permute-start(f32[2,48,1536]{2,1,0:T(8,128)S(1)} %get-tuple-element.210), channel_id=1, source_target_pairs={{0,8},{2,10},{4,12},{6,14},{8,0},{10,2},{12,4},{14,6},{16,24},{18,... | collective-permute-start | bytes 1769480 | tf_op jit(solution)/shard_map/ppermute | solution.py:784
  128.4 13.4 %collective-permute-start.20 = (f32[4,32,896]{2,1,0:T(8,128)S(1)}, f32[4,32,896]{2,1,0:T(8,128)S(1)}, u32[]{:S(2)}, u32[]{:S(2)}) collective-permute-start(f32[4,32,896]{2,1,0:T(8,128)S(1)} %get-tuple-element.211), channel_id=1, source_target_pairs={{0,4},{2,6},{4,0},{6,2},{8,12},{10,14},{12,8},{14,10},{16,20},{18,... | collective-permute-start | bytes 1376264 | tf_op jit(solution)/shard_map/ppermute | solution.py:784
  130.0 24.5 %collective-permute-start.18 = (f32[4,48,768]{2,1,0:T(8,128)S(1)}, f32[4,48,768]{2,1,0:T(8,128)S(1)}, u32[]{:S(2)}, u32[]{:S(2)}) collective-permute-start(f32[4,48,768]{2,1,0:T(8,128)S(1)} %get-tuple-element.209), channel_id=1, source_target_pairs={{0,4},{2,6},{4,0},{6,2},{8,12},{10,14},{12,8},{14,10},{16,20},{18,... | collective-permute-start | bytes 1769480 | tf_op jit(solution)/shard_map/ppermute | solution.py:784
  130.8 62.3 %collective-permute-start.22 = (f32[512,768]{1,0:T(8,128)S(1)}, f32[512,768]{1,0:T(8,128)S(1)}, u32[]{:S(2)}, u32[]{:S(2)}) collective-permute-start(f32[512,768]{1,0:T(8,128)S(1)} %hidden_grad.1.refs_10_.refs_2_), channel_id=1, source_target_pairs={{0,1},{1,0},{2,3},{3,2},{4,5},{5,4},{6,7},{7,6},{8,9},{9,8},{10,11... | collective-permute-start | bytes 4718600 | tf_op jit(solution)/shard_map/ppermute | solution.py:780
  131.4 29.2 %collective-permute-start.25 = (f32[2,48,1536]{2,1,0:T(8,128)S(1)}, f32[2,48,1536]{2,1,0:T(8,128)S(1)}, u32[]{:S(2)}, u32[]{:S(2)}) collective-permute-start(f32[2,48,1536]{2,1,0:T(8,128)S(1)} %get-tuple-element.219), channel_id=1, source_target_pairs={{0,16},{2,18},{4,20},{6,22},{8,24},{10,26},{12,28},{14,30},{16,0},... | collective-permute-start | bytes 1769480 | tf_op jit(solution)/shard_map/ppermute | solution.py:784
  141.8 28.7 %collective-permute-start.27 = (f32[4,48,768]{2,1,0:T(8,128)S(1)}, f32[4,48,768]{2,1,0:T(8,128)S(1)}, u32[]{:S(2)}, u32[]{:S(2)}) collective-permute-start(f32[4,48,768]{2,1,0:T(8,128)S(1)} %get-tuple-element.224), channel_id=1, source_target_pairs={{0,4},{2,6},{4,0},{6,2},{8,12},{10,14},{12,8},{14,10},{16,20},{18,... | collective-permute-start | bytes 1769480 | tf_op jit(solution)/shard_map/ppermute | solution.py:784
  148.5 11.2 %collective-permute-start.23 = (f32[2,32,896]{2,1,0:T(8,128)S(1)}, f32[2,32,896]{2,1,0:T(8,128)S(1)}, u32[]{:S(2)}, u32[]{:S(2)}) collective-permute-start(f32[2,32,896]{2,1,0:T(8,128)S(1)} %get-tuple-element.218), channel_id=1, source_target_pairs={{0,8},{2,10},{4,12},{6,14},{8,0},{10,2},{12,4},{14,6},{16,24},{18,... | collective-permute-start | bytes 688136 | tf_op jit(solution)/shard_map/ppermute | solution.py:784
  159.7 10.8 %collective-permute-start.24 = (f32[2,32,896]{2,1,0:T(8,128)S(1)}, f32[2,32,896]{2,1,0:T(8,128)S(1)}, u32[]{:S(2)}, u32[]{:S(2)}) collective-permute-start(f32[2,32,896]{2,1,0:T(8,128)S(1)} %rel_4.1.refs_2_.refs_0_), channel_id=1, source_target_pairs={{0,16},{2,18},{4,20},{6,22},{8,24},{10,26},{12,28},{14,30},{16,0},... | collective-permute-start | bytes 688136 | tf_op jit(solution)/shard_map/ppermute | solution.py:784
  160.6 17.8 %collective-permute-start.30 = (f32[1,48,1536]{2,1,0:T(8,128)S(1)}, f32[1,48,1536]{2,1,0:T(8,128)S(1)}, u32[]{:S(2)}, u32[]{:S(2)}) collective-permute-start(f32[1,48,1536]{2,1,0:T(8,128)S(1)} %get-tuple-element.227), channel_id=1, source_target_pairs={{0,4},{2,6},{4,0},{6,2},{8,12},{10,14},{12,8},{14,10},{16,20},{18,... | collective-permute-start | bytes 884744 | tf_op jit(solution)/shard_map/ppermute | solution.py:784
  176.5 12.6 %collective-permute-start.28 = (f32[2,32,896]{2,1,0:T(8,128)S(1)}, f32[2,32,896]{2,1,0:T(8,128)S(1)}, u32[]{:S(2)}, u32[]{:S(2)}) collective-permute-start(f32[2,32,896]{2,1,0:T(8,128)S(1)} %rel_join.1.refs_2_.refs_0_), channel_id=1, source_target_pairs={{0,8},{2,10},{4,12},{6,14},{8,0},{10,2},{12,4},{14,6},{16,24},{18,... | collective-permute-start | bytes 688136 | tf_op jit(solution)/shard_map/ppermute | solution.py:784
  190.0 13.8 %collective-permute-start.33 = (f32[4,32,896]{2,1,0:T(8,128)S(1)}, f32[4,32,896]{2,1,0:T(8,128)S(1)}, u32[]{:S(2)}, u32[]{:S(2)}) collective-permute-start(f32[4,32,896]{2,1,0:T(8,128)S(1)} %pack_4.1.refs_6_), channel_id=1, source_target_pairs={{0,4},{2,6},{4,0},{6,2},{8,12},{10,14},{12,8},{14,10},{16,20},{18,... | collective-permute-start | bytes 1376264 | tf_op jit(solution)/shard_map/ppermute | solution.py:784
  191.2 11.8 %collective-permute-start.34 = (f32[1,48,1536]{2,1,0:T(8,128)S(1)}, f32[1,48,1536]{2,1,0:T(8,128)S(1)}, u32[]{:S(2)}, u32[]{:S(2)}) collective-permute-start(f32[1,48,1536]{2,1,0:T(8,128)S(1)} %get-tuple-element.234), channel_id=1, source_target_pairs={{0,16},{2,18},{4,20},{6,22},{8,24},{10,26},{12,28},{14,30},{16,0},... | collective-permute-start | bytes 884744 | tf_op jit(solution)/shard_map/ppermute | solution.py:784
  (56 other events, 453.6 us)

commit v2 on v1

--- a/solution.py
+++ b/solution.py
@@ -18,7 +18,7 @@
 LANES = 128
 STREAMS = 2
 CONTEXTS = 1
-TAIL = "LYKGDIR(VQ)RDVXISQJiQqP(VH)dP(vU)"
+TAIL = "LYKGDIR(VQ)RDVXI(SQ)JiQqP(VH)dP(vU)"
 REL_PIECES = 2
 HEAD_PIECES = 1
 QUARTERS = 4

time: 216 us -> 216 us (level)
    pallas_call x40 -> x39, Pallas kernels: 77.3 us -> 77.3 us  [call(): pl.pallas_call(body, in_specs=in_specs, out_specs=[pl.BlockSpec() if at i...]
  transfers between devices with their start and end apart: 36 -> 36, of which waited for: 19 -> 20; matrix products, arithmetic and copies ran while one was open for 0% -> 0% of each run, Pallas kernels for 33% -> 33%
where the time goes in v2:
time: 216 us
  waiting for transfers between devices  103 us (48%)
  Pallas kernels  77.3 us (36%)
  starting transfers between devices  30.6 us (14%)
  local copies, waits for them, and re-layouts  3.07 us (1%)
  between operations  2.28 us (1%)
    pallas_call x39, Pallas kernels, call(): pl.pallas_call(body, in_specs=in_specs, out_specs=[pl.BlockSpec() if at i...  77.3 us
    ppermute x27, waiting for transfers between devices, flip(): return lax.ppermute(value, 'dp', [(i, i ^ bit) for i in range(parts)])  59.7 us
    ppermute x9, waiting for transfers between devices, swap_head(): return lax.ppermute(value, 'head', [(0, 1), (1, 0)])  42.9 us
    ppermute x27, starting transfers between devices, flip(): return lax.ppermute(value, 'dp', [(i, i ^ bit) for i in range(parts)])  22.2 us
    ppermute x9, starting transfers between devices, swap_head(): return lax.ppermute(value, 'head', [(0, 1), (1, 0)])  8.4 us
  transfers between devices with their start and end apart: 36, of which 20 were waited for; matrix products, arithmetic and copies ran while one was open for 0% of the time, Pallas kernels for 33%

profile of v2, /device:TPU:0, one launch (start us, length us, event | category | flops | bytes accessed | tf_op | source)
XLA Modules:
  0.0 215.9 jit_solution(10680232903044767373)
XLA Ops:
  0.7 5.0 %project.1 = (bf16[512,384]{1,0:T(8,128)(2,1)S(1)}, bf16[512,384]{1,0:T(8,128)(2,1)S(1)}, bf16[512,384]{1,0:T(8,128)(2,1)S(1)}, bf16[1024,384]{1,0:T(8,128)(2,1)...) custom-call(s32[1,1024]{1,0:T(1,128)} %constant.2.clone.refs_0_, bf16[512,768]{1,0:T(8,128)(2,1)} %refs_0_.7, ...), custom_call_target="tpu_custom_call" | custom-call | flops 1024 | bytes 1024 | tf_op jit(solution)/shard_map/project/pallas_call | solution.py:87
  5.7 3.0 %collective-permute-start = (f32[96,768]{1,0:T(8,128)S(1)}, f32[96,768]{1,0:T(8,128)S(1)}, u32[]{:S(2)}, u32[]{:S(2)}) collective-permute-start(f32[96,768]{1,0:T(8,128)S(1)} %get-tuple-element.134.refs_6_), channel_id=1, source_target_pairs={{0,1},{1,0},{2,3},{3,2},{4,5},{5,4},{6,7},{7,6},{8,9},{9,8},{10,11... | collective-permute-start | bytes 884744 | tf_op jit(solution)/shard_map/ppermute | solution.py:780
  9.4 7.2 %attend_0.1 = (f32[256,384]{1,0:T(8,128)S(1)}, bf16[6,256,512]{2,1,0:T(8,128)(2,1)S(1)}) custom-call(s32[1]{0:T(128)S(6)} %copy.48.refs_0_, bf16[512,384]{1,0:T(8,128)(2,1)S(1)} %get-tuple-element.135.refs_1_, bf16[512,384]{1,0:T(8,128)(2,1)S(1)} %get-tuple-element.136.refs_2_, bf16[512,384]{1,0:T(8,128)(2,1)S(1)} %get-tuple-element.137.refs_3_, ...), custom_call_target="tpu_custom_call" | custom-call | flops 1024 | bytes 1024 | tf_op jit(solution)/shard_map/attend_0/pallas_call | solution.py:87
  19.0 7.0 %attend_1.1 = (f32[256,384]{1,0:T(8,128)S(1)}, bf16[6,256,512]{2,1,0:T(8,128)(2,1)S(1)}) custom-call(s32[1]{0:T(128)S(6)} %copy.48.refs_0_, bf16[512,384]{1,0:T(8,128)(2,1)S(1)} %get-tuple-element.135.refs_1_, bf16[512,384]{1,0:T(8,128)(2,1)S(1)} %get-tuple-element.136.refs_2_, bf16[512,384]{1,0:T(8,128)(2,1)S(1)} %get-tuple-element.137.refs_3_, ...), custom_call_target="tpu_custom_call" | custom-call | flops 1024 | bytes 1024 | tf_op jit(solution)/shard_map/attend_1/pallas_call | solution.py:87
  29.6 3.1 %feed_0.1 = (f32[256,768]{1,0:T(8,128)S(1)}, f32[256,1]{1,0:T(8,128)S(1)}, bf16[256,768]{1,0:T(8,128)(2,1)S(1)}, bf16[256,1536]{1,0:T(8,128)(2,1)S(1)}, f32[256,1536]{1,0:T(8,128)S(1)}, /*index=5*/f32[256,768]{1,0:T(8,128)S(1)}) custom-call(bf16[768,768]{1,0:T(8,128)(2,1)S(1)} %bitcast.4, bf16[768]{0:T(1024)(128)(2,1)S(1)} %copy-done.43, ...), custom_call_target="tpu_custom_call" | custom-call | flops 1024 | bytes 1024 | tf_op jit(solution)/shard_map/feed_0/pallas_call | solution.py:87
  33.6 4.6 %collective-permute-done.4.refs_9_ = f32[256,384]{1,0:T(8,128)S(1)} collective-permute-done((f32[256,384]{1,0:T(8,128)S(1)}, f32[256,384]{1,0:T(8,128)S(1)}, u32[]{:S(2)}, u32[]{:S(2)}) %collective-permute-start.4) | collective-permute-done | bytes 393248 | tf_op jit(solution)/shard_map/ppermute | solution.py:780
  38.3 3.1 %feed_1.1 = (f32[256,768]{1,0:T(8,128)S(1)}, f32[256,1]{1,0:T(8,128)S(1)}, bf16[256,768]{1,0:T(8,128)(2,1)S(1)}, bf16[256,1536]{1,0:T(8,128)(2,1)S(1)}, f32[256,1536]{1,0:T(8,128)S(1)}, /*index=5*/f32[256,768]{1,0:T(8,128)S(1)}) custom-call(bf16[768,768]{1,0:T(8,128)(2,1)S(1)} %bitcast.5, bf16[768]{0:T(1024)(128)(2,1)S(1)} %copy-done.43, ...), custom_call_target="tpu_custom_call" | custom-call | flops 68719476736 | bytes 1024 | tf_op jit(solution)/shard_map/feed_1/pallas_call | solution.py:87
  41.7 13.4 %collective-permute-done.7.refs_1_ = f32[256,768]{1,0:T(8,128)S(1)} collective-permute-done((f32[256,768]{1,0:T(8,128)S(1)}, f32[256,768]{1,0:T(8,128)S(1)}, u32[]{:S(2)}, u32[]{:S(2)}) %collective-permute-start.7) | collective-permute-done | bytes 786464 | tf_op jit(solution)/shard_map/ppermute | solution.py:780
  55.1 3.1 %feed_back_0.1 = (bf16[256,768]{1,0:T(8,128)(2,1)S(1)}, f32[256,768]{1,0:T(8,128)S(1)}, bf16[256,768]{1,0:T(8,128)(2,1)S(1)}, bf16[256,1536]{1,0:T(8,128)(2,1)S(...) custom-call(f32[256,768]{1,0:T(8,128)S(1)} %get-tuple-element.148.refs_0_, ...), custom_call_target="tpu_custom_call" | custom-call | flops 1024 | bytes 1024 | tf_op jit(solution)/shard_map/feed_back_0/pallas_call | solution.py:87
  58.6 13.4 %collective-permute-done.6.refs_1_ = f32[256,768]{1,0:T(8,128)S(1)} collective-permute-done((f32[256,768]{1,0:T(8,128)S(1)}, f32[256,768]{1,0:T(8,128)S(1)}, u32[]{:S(2)}, u32[]{:S(2)}) %collective-permute-start.6) | collective-permute-done | bytes 786464 | tf_op jit(solution)/shard_map/ppermute | solution.py:780
  72.0 3.8 %feed_back_1.1 = (bf16[512,768]{1,0:T(8,128)(2,1)}, f32[256,768]{1,0:T(8,128)S(1)}, bf16[256,768]{1,0:T(8,128)(2,1)S(1)}, bf16[256,1536]{1,0:T(8,128)(2,1)S(1)},...) custom-call(f32[256,768]{1,0:T(8,128)S(1)} %get-tuple-element.145.refs_0_, ...), custom_call_target="tpu_custom_call" | custom-call | flops 1024 | bytes 1024 | tf_op jit(solution)/shard_map/feed_back_1/pallas_call | solution.py:87
  82.3 6.5 %collective-permute-done.9.refs_1_ = f32[256,768]{1,0:T(8,128)S(1)} collective-permute-done((f32[256,768]{1,0:T(8,128)S(1)}, f32[256,768]{1,0:T(8,128)S(1)}, u32[]{:S(2)}, u32[]{:S(2)}) %collective-permute-start.9) | collective-permute-done | bytes 786464 | tf_op jit(solution)/shard_map/ppermute | solution.py:780
  94.4 9.7 %attend_back_0.1 = (bf16[256,384]{1,0:T(8,128)(2,1)S(1)}, f32[512,384]{1,0:T(8,128)S(1)}, f32[512,384]{1,0:T(8,128)S(1)}, f32[1024,384]{1,0:T(8,128)S(1)}, f32[1024,384]{1,0:T(8,128)S(1)}) custom-call(bf16[256,384]{1,0:T(8,128)(2,1)S(1)} %get-tuple-element.170.refs_0_, bf16[512,384]{1,0:T(8,128)(2,1)S(1)} %copy-done.18, bf16[512,384]{1,0:T(8,128)(2,1)S(1)} %copy-done.20, ...), custom_call_target="tpu_custom_call" | custom-call | flops 68719476736 | bytes 1024 | tf_op jit(solution)/shard_map/attend_back_0/pallas_call | solution.py:87
  105.2 9.5 %attend_back_1.1 = (bf16[256,384]{1,0:T(8,128)(2,1)S(1)}, f32[512,384]{1,0:T(8,128)S(1)}, f32[512,384]{1,0:T(8,128)S(1)}, f32[1024,384]{1,0:T(8,128)S(1)}, f32[1...) custom-call(bf16[256,384]{1,0:T(8,128)(2,1)S(1)} %get-tuple-element., ...), custom_call_target="tpu_custom_call", output_to_operand_aliasing={{1}: (7, {}), {2}: (8, {}), {3}: (9, {}), {4}: (10, {})} | custom-call | flops 68719476736 | bytes 1024 | tf_op jit(solution)/shard_map/attend_back_1/pallas_call | solution.py:87
  134.0 7.9 %collective-permute-done.20.refs_1_ = f32[4,32,896]{2,1,0:T(8,128)S(1)} collective-permute-done((f32[4,32,896]{2,1,0:T(8,128)S(1)}, f32[4,32,896]{2,1,0:T(8,128)S(1)}, u32[]{:S(2)}, u32[]{:S(2)}) %collective-permute-start.20) | collective-permute-done | bytes 458784 | tf_op jit(solution)/shard_map/ppermute | solution.py:784
  143.2 5.3 %collective-permute-done.19.refs_1_ = f32[2,48,1536]{2,1,0:T(8,128)S(1)} collective-permute-done((f32[2,48,1536]{2,1,0:T(8,128)S(1)}, f32[2,48,1536]{2,1,0:T(8,128)S(1)}, u32[]{:S(2)}, u32[]{:S(2)}) %collective-permute-start.19) | collective-permute-done | bytes 589856 | tf_op jit(solution)/shard_map/ppermute | solution.py:784
  148.5 6.0 %collective-permute-done.18.refs_1_ = f32[4,48,768]{2,1,0:T(8,128)S(1)} collective-permute-done((f32[4,48,768]{2,1,0:T(8,128)S(1)}, f32[4,48,768]{2,1,0:T(8,128)S(1)}, u32[]{:S(2)}, u32[]{:S(2)}) %collective-permute-start.18) | collective-permute-done | bytes 589856 | tf_op jit(solution)/shard_map/ppermute | solution.py:784
  154.6 5.1 %collective-permute-done.23.refs_1_ = f32[2,32,896]{2,1,0:T(8,128)S(1)} collective-permute-done((f32[2,32,896]{2,1,0:T(8,128)S(1)}, f32[2,32,896]{2,1,0:T(8,128)S(1)}, u32[]{:S(2)}, u32[]{:S(2)}) %collective-permute-start.23) | collective-permute-done | bytes 229408 | tf_op jit(solution)/shard_map/ppermute | solution.py:784
  162.0 5.1 %collective-permute-done.25.refs_3_ = f32[4,48,768]{2,1,0:T(8,128)S(1)} collective-permute-done((f32[4,48,768]{2,1,0:T(8,128)S(1)}, f32[4,48,768]{2,1,0:T(8,128)S(1)}, u32[]{:S(2)}, u32[]{:S(2)}) %collective-permute-start.25) | collective-permute-done | bytes 589856 | tf_op jit(solution)/shard_map/ppermute | solution.py:784
  167.1 3.3 %collective-permute-done.24.refs_1_ = f32[2,32,896]{2,1,0:T(8,128)S(1)} collective-permute-done((f32[2,32,896]{2,1,0:T(8,128)S(1)}, f32[2,32,896]{2,1,0:T(8,128)S(1)}, u32[]{:S(2)}, u32[]{:S(2)}) %collective-permute-start.24) | collective-permute-done | bytes 229408 | tf_op jit(solution)/shard_map/ppermute | solution.py:784
  171.8 4.7 %collective-permute-done.27.refs_1_ = f32[2,32,768]{2,1,0:T(8,128)S(1)} collective-permute-done((f32[2,32,768]{2,1,0:T(8,128)S(1)}, f32[2,32,768]{2,1,0:T(8,128)S(1)}, u32[]{:S(2)}, u32[]{:S(2)}) %collective-permute-start.27) | collective-permute-done | bytes 196640 | tf_op jit(solution)/shard_map/ppermute | solution.py:780
  181.5 6.9 %collective-permute-done.31.refs_1_ = f32[1,48,768]{2,1,0:T(8,128)S(1)} collective-permute-done((f32[1,48,768]{2,1,0:T(8,128)S(1)}, f32[1,48,768]{2,1,0:T(8,128)S(1)}, u32[]{:S(2)}, u32[]{:S(2)}) %collective-permute-start.31) | collective-permute-done | bytes 147488 | tf_op jit(solution)/shard_map/ppermute | solution.py:784
  193.1 7.9 %collective-permute-done.21.refs_1_ = f32[2,48,768]{2,1,0:T(8,128)S(1)} collective-permute-done((f32[2,48,768]{2,1,0:T(8,128)S(1)}, f32[2,48,768]{2,1,0:T(8,128)S(1)}, u32[]{:S(2)}, u32[]{:S(2)}) %collective-permute-start.21) | collective-permute-done | bytes 294944 | tf_op jit(solution)/shard_map/ppermute | solution.py:784
  205.3 8.9 %collective-permute-done.32.refs_1_ = f32[1,48,768]{2,1,0:T(8,128)S(1)} collective-permute-done((f32[1,48,768]{2,1,0:T(8,128)S(1)}, f32[1,48,768]{2,1,0:T(8,128)S(1)}, u32[]{:S(2)}, u32[]{:S(2)}) %collective-permute-start.32) | collective-permute-done | bytes 147488 | tf_op jit(solution)/shard_map/ppermute | solution.py:784
  (176 shorter events, 60.0 us)
Async XLA Ops:
  5.7 10.9 %collective-permute-start = (f32[96,768]{1,0:T(8,128)S(1)}, f32[96,768]{1,0:T(8,128)S(1)}, u32[]{:S(2)}, u32[]{:S(2)}) collective-permute-start(f32[96,768]{1,0:T(8,128)S(1)} %get-tuple-element.134.refs_6_), channel_id=1, source_target_pairs={{0,1},{1,0},{2,3},{3,2},{4,5},{5,4},{6,7},{7,6},{8,9},{9,8},{10,11... | collective-permute-start | bytes 884744 | tf_op jit(solution)/shard_map/ppermute | solution.py:780
  16.6 10.8 %collective-permute-start.2 = (f32[96,768]{1,0:T(8,128)S(1)}, f32[96,768]{1,0:T(8,128)S(1)}, u32[]{:S(2)}, u32[]{:S(2)}) collective-permute-start(f32[96,768]{1,0:T(8,128)S(1)} %collective-permute-done.refs_1_), channel_id=1, source_target_pairs={{0,4},{2,6},{4,0},{6,2},{8,12},{10,14},{12,8},{14,10},{16,20},{18,... | collective-permute-start | bytes 884744 | tf_op jit(solution)/shard_map/ppermute | solution.py:784
  18.2 11.3 %collective-permute-start.5 = (f32[256,384]{1,0:T(8,128)S(1)}, f32[256,384]{1,0:T(8,128)S(1)}, u32[]{:S(2)}, u32[]{:S(2)}) collective-permute-start(f32[256,384]{1,0:T(8,128)S(1)} %get-tuple-element.143.refs_6_.refs_8_.refs_3_), channel_id=1, source_target_pairs={{0,1},{1,0},{2,3},{3,2},{4,5},{5,4},{6,7},{7,6},{8,9},{9,8},{10,11... | collective-permute-start | bytes 1179656 | tf_op jit(solution)/shard_map/ppermute | solution.py:780
  26.1 12.1 %collective-permute-start.4 = (f32[256,384]{1,0:T(8,128)S(1)}, f32[256,384]{1,0:T(8,128)S(1)}, u32[]{:S(2)}, u32[]{:S(2)}) collective-permute-start(f32[256,384]{1,0:T(8,128)S(1)} %get-tuple-element.142.refs_5_.refs_8_), channel_id=1, source_target_pairs={{0,1},{1,0},{2,3},{3,2},{4,5},{5,4},{6,7},{7,6},{8,9},{9,8},{10,11... | collective-permute-start | bytes 1179656 | tf_op jit(solution)/shard_map/ppermute | solution.py:780
  32.7 22.4 %collective-permute-start.7 = (f32[256,768]{1,0:T(8,128)S(1)}, f32[256,768]{1,0:T(8,128)S(1)}, u32[]{:S(2)}, u32[]{:S(2)}) collective-permute-start(f32[256,768]{1,0:T(8,128)S(1)} %get-tuple-element.148.refs_0_), channel_id=1, source_target_pairs={{0,1},{1,0},{2,3},{3,2},{4,5},{5,4},{6,7},{7,6},{8,9},{9,8},{10,11... | collective-permute-start | bytes 2359304 | tf_op jit(solution)/shard_map/ppermute | solution.py:780
  41.4 30.5 %collective-permute-start.6 = (f32[256,768]{1,0:T(8,128)S(1)}, f32[256,768]{1,0:T(8,128)S(1)}, u32[]{:S(2)}, u32[]{:S(2)}) collective-permute-start(f32[256,768]{1,0:T(8,128)S(1)} %get-tuple-element.145.refs_0_), channel_id=1, source_target_pairs={{0,1},{1,0},{2,3},{3,2},{4,5},{5,4},{6,7},{7,6},{8,9},{9,8},{10,11... | collective-permute-start | bytes 2359304 | tf_op jit(solution)/shard_map/ppermute | solution.py:780
  58.3 30.5 %collective-permute-start.9 = (f32[256,768]{1,0:T(8,128)S(1)}, f32[256,768]{1,0:T(8,128)S(1)}, u32[]{:S(2)}, u32[]{:S(2)}) collective-permute-start(f32[256,768]{1,0:T(8,128)S(1)} %get-tuple-element.157.refs_0_), channel_id=1, source_target_pairs={{0,1},{1,0},{2,3},{3,2},{4,5},{5,4},{6,7},{7,6},{8,9},{9,8},{10,11... | collective-permute-start | bytes 2359304 | tf_op jit(solution)/shard_map/ppermute | solution.py:780
  78.5 11.2 %collective-permute-start.11 = (f32[8,48,1536]{2,1,0:T(8,128)S(1)}, f32[8,48,1536]{2,1,0:T(8,128)S(1)}, u32[]{:S(2)}, u32[]{:S(2)}) collective-permute-start(f32[8,48,1536]{2,1,0:T(8,128)S(1)} %get-tuple-element.173), channel_id=1, source_target_pairs={{0,2},{2,0},{4,6},{6,4},{8,10},{10,8},{12,14},{14,12},{16,18},{18,... | collective-permute-start | bytes 7077896 | tf_op jit(solution)/shard_map/ppermute | solution.py:784
  81.5 9.9 %collective-permute-start.10 = (f32[8,48,1536]{2,1,0:T(8,128)S(1)}, f32[8,48,1536]{2,1,0:T(8,128)S(1)}, u32[]{:S(2)}, u32[]{:S(2)}) collective-permute-start(f32[8,48,1536]{2,1,0:T(8,128)S(1)} %get-tuple-element.172), channel_id=1, source_target_pairs={{0,2},{2,0},{4,6},{6,4},{8,10},{10,8},{12,14},{14,12},{16,18},{18,... | collective-permute-start | bytes 7077896 | tf_op jit(solution)/shard_map/ppermute | solution.py:784
  82.1 22.2 %collective-permute-start.8 = (f32[256,768]{1,0:T(8,128)S(1)}, f32[256,768]{1,0:T(8,128)S(1)}, u32[]{:S(2)}, u32[]{:S(2)}) collective-permute-start(f32[256,768]{1,0:T(8,128)S(1)} %get-tuple-element.155.refs_0_), channel_id=1, source_target_pairs={{0,1},{1,0},{2,3},{3,2},{4,5},{5,4},{6,7},{7,6},{8,9},{9,8},{10,11... | collective-permute-start | bytes 2359304 | tf_op jit(solution)/shard_map/ppermute | solution.py:780
  90.9 32.1 %collective-permute-start.17 = (f32[4,48,1536]{2,1,0:T(8,128)}, f32[4,48,1536]{2,1,0:T(8,128)}, u32[]{:S(2)}, u32[]{:S(2)}) collective-permute-start(f32[4,48,1536]{2,1,0:T(8,128)} %get-tuple-element.204), channel_id=1, source_target_pairs={{0,4},{2,6},{4,0},{6,2},{8,12},{10,14},{12,8},{14,10},{16,20},{18,... | collective-permute-start | bytes 3538952 | tf_op jit(solution)/shard_map/ppermute | solution.py:784
  92.8 32.1 %collective-permute-start.16 = (f32[4,48,1536]{2,1,0:T(8,128)}, f32[4,48,1536]{2,1,0:T(8,128)}, u32[]{:S(2)}, u32[]{:S(2)}) collective-permute-start(f32[4,48,1536]{2,1,0:T(8,128)} %get-tuple-element.203), channel_id=1, source_target_pairs={{0,8},{2,10},{4,12},{6,14},{8,0},{10,2},{12,4},{14,6},{16,24},{18,... | collective-permute-start | bytes 3538952 | tf_op jit(solution)/shard_map/ppermute | solution.py:784
  124.9 23.6 %collective-permute-start.19 = (f32[2,48,1536]{2,1,0:T(8,128)S(1)}, f32[2,48,1536]{2,1,0:T(8,128)S(1)}, u32[]{:S(2)}, u32[]{:S(2)}) collective-permute-start(f32[2,48,1536]{2,1,0:T(8,128)S(1)} %get-tuple-element.210), channel_id=1, source_target_pairs={{0,8},{2,10},{4,12},{6,14},{8,0},{10,2},{12,4},{14,6},{16,24},{18,... | collective-permute-start | bytes 1769480 | tf_op jit(solution)/shard_map/ppermute | solution.py:784
  128.4 13.4 %collective-permute-start.20 = (f32[4,32,896]{2,1,0:T(8,128)S(1)}, f32[4,32,896]{2,1,0:T(8,128)S(1)}, u32[]{:S(2)}, u32[]{:S(2)}) collective-permute-start(f32[4,32,896]{2,1,0:T(8,128)S(1)} %get-tuple-element.211), channel_id=1, source_target_pairs={{0,4},{2,6},{4,0},{6,2},{8,12},{10,14},{12,8},{14,10},{16,20},{18,... | collective-permute-start | bytes 1376264 | tf_op jit(solution)/shard_map/ppermute | solution.py:784
  130.0 24.5 %collective-permute-start.18 = (f32[4,48,768]{2,1,0:T(8,128)S(1)}, f32[4,48,768]{2,1,0:T(8,128)S(1)}, u32[]{:S(2)}, u32[]{:S(2)}) collective-permute-start(f32[4,48,768]{2,1,0:T(8,128)S(1)} %get-tuple-element.209), channel_id=1, source_target_pairs={{0,4},{2,6},{4,0},{6,2},{8,12},{10,14},{12,8},{14,10},{16,20},{18,... | collective-permute-start | bytes 1769480 | tf_op jit(solution)/shard_map/ppermute | solution.py:784
  130.8 62.3 %collective-permute-start.22 = (f32[512,768]{1,0:T(8,128)S(1)}, f32[512,768]{1,0:T(8,128)S(1)}, u32[]{:S(2)}, u32[]{:S(2)}) collective-permute-start(f32[512,768]{1,0:T(8,128)S(1)} %hidden_grad.1.refs_10_.refs_2_), channel_id=1, source_target_pairs={{0,1},{1,0},{2,3},{3,2},{4,5},{5,4},{6,7},{7,6},{8,9},{9,8},{10,11... | collective-permute-start | bytes 4718600 | tf_op jit(solution)/shard_map/ppermute | solution.py:780
  131.4 29.2 %collective-permute-start.26 = (f32[2,48,1536]{2,1,0:T(8,128)S(1)}, f32[2,48,1536]{2,1,0:T(8,128)S(1)}, u32[]{:S(2)}, u32[]{:S(2)}) collective-permute-start(f32[2,48,1536]{2,1,0:T(8,128)S(1)} %get-tuple-element.221), channel_id=1, source_target_pairs={{0,16},{2,18},{4,20},{6,22},{8,24},{10,26},{12,28},{14,30},{16,0},... | collective-permute-start | bytes 1769480 | tf_op jit(solution)/shard_map/ppermute | solution.py:784
  141.9 25.3 %collective-permute-start.25 = (f32[4,48,768]{2,1,0:T(8,128)S(1)}, f32[4,48,768]{2,1,0:T(8,128)S(1)}, u32[]{:S(2)}, u32[]{:S(2)}) collective-permute-start(f32[4,48,768]{2,1,0:T(8,128)S(1)} %get-tuple-element.220), channel_id=1, source_target_pairs={{0,4},{2,6},{4,0},{6,2},{8,12},{10,14},{12,8},{14,10},{16,20},{18,... | collective-permute-start | bytes 1769480 | tf_op jit(solution)/shard_map/ppermute | solution.py:784
  148.5 11.2 %collective-permute-start.23 = (f32[2,32,896]{2,1,0:T(8,128)S(1)}, f32[2,32,896]{2,1,0:T(8,128)S(1)}, u32[]{:S(2)}, u32[]{:S(2)}) collective-permute-start(f32[2,32,896]{2,1,0:T(8,128)S(1)} %get-tuple-element.218), channel_id=1, source_target_pairs={{0,8},{2,10},{4,12},{6,14},{8,0},{10,2},{12,4},{14,6},{16,24},{18,... | collective-permute-start | bytes 688136 | tf_op jit(solution)/shard_map/ppermute | solution.py:784
  159.7 10.8 %collective-permute-start.24 = (f32[2,32,896]{2,1,0:T(8,128)S(1)}, f32[2,32,896]{2,1,0:T(8,128)S(1)}, u32[]{:S(2)}, u32[]{:S(2)}) collective-permute-start(f32[2,32,896]{2,1,0:T(8,128)S(1)} %rel_4.1.refs_2_.refs_0_), channel_id=1, source_target_pairs={{0,16},{2,18},{4,20},{6,22},{8,24},{10,26},{12,28},{14,30},{16,0},... | collective-permute-start | bytes 688136 | tf_op jit(solution)/shard_map/ppermute | solution.py:784
  160.6 17.8 %collective-permute-start.30 = (f32[1,48,1536]{2,1,0:T(8,128)S(1)}, f32[1,48,1536]{2,1,0:T(8,128)S(1)}, u32[]{:S(2)}, u32[]{:S(2)}) collective-permute-start(f32[1,48,1536]{2,1,0:T(8,128)S(1)} %get-tuple-element.227), channel_id=1, source_target_pairs={{0,4},{2,6},{4,0},{6,2},{8,12},{10,14},{12,8},{14,10},{16,20},{18,... | collective-permute-start | bytes 884744 | tf_op jit(solution)/shard_map/ppermute | solution.py:784
  176.5 12.6 %collective-permute-start.28 = (f32[2,32,896]{2,1,0:T(8,128)S(1)}, f32[2,32,896]{2,1,0:T(8,128)S(1)}, u32[]{:S(2)}, u32[]{:S(2)}) collective-permute-start(f32[2,32,896]{2,1,0:T(8,128)S(1)} %rel_join.1.refs_2_.refs_0_), channel_id=1, source_target_pairs={{0,8},{2,10},{4,12},{6,14},{8,0},{10,2},{12,4},{14,6},{16,24},{18,... | collective-permute-start | bytes 688136 | tf_op jit(solution)/shard_map/ppermute | solution.py:784
  190.0 13.8 %collective-permute-start.33 = (f32[4,32,896]{2,1,0:T(8,128)S(1)}, f32[4,32,896]{2,1,0:T(8,128)S(1)}, u32[]{:S(2)}, u32[]{:S(2)}) collective-permute-start(f32[4,32,896]{2,1,0:T(8,128)S(1)} %pack_4.1.refs_6_), channel_id=1, source_target_pairs={{0,4},{2,6},{4,0},{6,2},{8,12},{10,14},{12,8},{14,10},{16,20},{18,... | collective-permute-start | bytes 1376264 | tf_op jit(solution)/shard_map/ppermute | solution.py:784
  191.3 11.8 %collective-permute-start.34 = (f32[1,48,1536]{2,1,0:T(8,128)S(1)}, f32[1,48,1536]{2,1,0:T(8,128)S(1)}, u32[]{:S(2)}, u32[]{:S(2)}) collective-permute-start(f32[1,48,1536]{2,1,0:T(8,128)S(1)} %get-tuple-element.234), channel_id=1, source_target_pairs={{0,16},{2,18},{4,20},{6,22},{8,24},{10,26},{12,28},{14,30},{16,0},... | collective-permute-start | bytes 884744 | tf_op jit(solution)/shard_map/ppermute | solution.py:784
  (56 other events, 453.4 us)
